TPU v7x, 256 devices: a whole 4x4x8 slice. The times are simulated.
256 devices in a mesh: segment: 4 (over z_hi), dp: 4 (over x), expert: 16 (over y, z_lo, core).
Axes of the slice: x: 4, y: 4, z: 8 (z_hi: 4, z_lo: 2; z = z_hi * 2 + z_lo), core: 2. Of those that a mesh axis runs over, the one named last changes fastest.
Arguments:
- fwd_inputs: bfloat16 [4, 4096, 2048], P('segment', ('dp', 'expert')), may hold values from -17 to 17
- fwd_routes: int32 [4, 4096, 8], P('segment', ('dp', 'expert')), may hold values from 0 to 127, as said below
- fwd_weights: float32 [4, 4096, 8], P('segment', ('dp', 'expert')), may hold values from 0.2 to 0.6
- bwd_inputs: bfloat16 [4, 4096, 2048], P('segment', ('dp', 'expert')), may hold values from -17 to 17
- bwd_cotangent: bfloat16 [4, 4096, 2048], P('segment', ('dp', 'expert')), may hold values from -6 to 6
- bwd_routes: int32 [4, 4096, 8], P('segment', ('dp', 'expert')), may hold values from 0 to 127, as said below
- bwd_weights: float32 [4, 4096, 8], P('segment', ('dp', 'expert')), may hold values from 0.2 to 0.6
- norm_gain: float32 [4, 2048], P('segment'), may hold values from 0.5 to 2
- w_gate: bfloat16 [4, 128, 2048, 384], P('segment', ('dp', 'expert')), may hold values from -0.125 to 0.125
- w_up: bfloat16 [4, 128, 2048, 384], P('segment', ('dp', 'expert')), may hold values from -0.125 to 0.125
- w_down: bfloat16 [4, 128, 384, 2048], P('segment', ('dp', 'expert')), may hold values from -0.3125 to 0.3125
Outputs:
- next_forward: bfloat16 [4, 4096, 2048], P('segment', ('dp', 'expert'))
- prev_grad: bfloat16 [4, 4096, 2048], P('segment', ('dp', 'expert'))
Inputs may be any that keep to these rules, and one draw needn't show every extreme that they name: `fwd_routes`: each row names 8 different experts. Among the rows of one device no expert is named more than 5 times, and in each section one expert is named exactly 5 times on every device of that section. `bwd_routes`: each row names 8 different experts. Among the rows of one device no expert is named more than 5 times, and in each section one expert is named exactly 5 times on every device of that section.
All inputs are finite; a program needn't handle non-finite values.
Results may differ from a plain program's by a relative error of at most 0.0059.
Values may be sent and summed in bfloat16 or wider, within the bound.
No kernel may reach another device: no remote copies, remote signals or barrier semaphores. Data moves between devices by JAX's collectives and lax.ppermute only.
A program may use at most 128 MiB of HBM per device.

v0:
```python
import jax
import jax.numpy as jnp
from jax import lax
from jax.sharding import PartitionSpec as P

EPSILON = 1e-06


def from_behind(value, axis, steps):
    count = lax.axis_size(axis)
    pairs = [(source, (source + steps) % count) for source in range(count)]
    return lax.ppermute(value, axis, pairs)


def normalize(inputs, norm_scale):
    values = inputs.astype(jnp.float32)
    inv_rms = lax.rsqrt(jnp.mean(values * values, axis=-1, keepdims=True) + EPSILON)
    return ((values * inv_rms * norm_scale).astype(jnp.bfloat16), values, inv_rms)


def slot_of(routes, experts_total, capacity):
    flat_routes = routes.reshape(-1)
    onehot = (flat_routes[:, None] == jnp.arange(experts_total, dtype=jnp.int32)[None, :]).astype(
        jnp.int32
    )
    before = jnp.cumsum(onehot, axis=0) - onehot
    position = jnp.sum(before * onehot, axis=1)
    return flat_routes * capacity + position


def pack(rows, slots, slot_total, top_count):
    row_count = rows.shape[0]
    source = jnp.arange(slots.shape[0], dtype=jnp.int32) // top_count
    owners = jnp.full((slot_total,), row_count, jnp.int32).at[slots].set(source)
    padded = jnp.concatenate([rows, jnp.zeros((1, rows.shape[1]), rows.dtype)], axis=0)
    return padded[owners]


def expert_work(fwd_rows, back_rows, cotangent_rows, gate_mat, up_mat, down_mat):
    gate_proj = jnp.einsum("gecd,edf->gecf", fwd_rows, gate_mat, preferred_element_type=jnp.float32)
    up_proj = jnp.einsum("gecd,edf->gecf", fwd_rows, up_mat, preferred_element_type=jnp.float32)
    activated = (gate_proj * jax.nn.sigmoid(gate_proj) * up_proj).astype(jnp.bfloat16)
    out_rows = jnp.einsum(
        "gecf,efd->gecd", activated, down_mat, preferred_element_type=jnp.float32
    ).astype(jnp.bfloat16)
    gate_back = jnp.einsum(
        "gecd,edf->gecf", back_rows, gate_mat, preferred_element_type=jnp.float32
    )
    up_back = jnp.einsum("gecd,edf->gecf", back_rows, up_mat, preferred_element_type=jnp.float32)
    back_hidden = jnp.einsum(
        "gecd,efd->gecf", cotangent_rows, down_mat, preferred_element_type=jnp.float32
    )
    sigmoid_gate = jax.nn.sigmoid(gate_back)
    d_gate = (
        back_hidden * up_back * sigmoid_gate * (1.0 + gate_back * (1.0 - sigmoid_gate))
    ).astype(jnp.bfloat16)
    d_up = (back_hidden * gate_back * sigmoid_gate).astype(jnp.bfloat16)
    d_normed = (
        jnp.einsum("gecf,edf->gecd", d_gate, gate_mat, preferred_element_type=jnp.float32)
        + jnp.einsum("gecf,edf->gecd", d_up, up_mat, preferred_element_type=jnp.float32)
    ).astype(jnp.bfloat16)
    return (out_rows, d_normed)


def body(
    fwd_inputs,
    fwd_routes,
    fwd_weights,
    bwd_inputs,
    bwd_cotangent,
    bwd_routes,
    bwd_weights,
    norm_gain,
    w_gate,
    w_up,
    w_down,
):
    inputs = fwd_inputs[0]
    tokens = inputs.shape[0]
    model_width = inputs.shape[1]
    top_count = fwd_routes.shape[2]
    groups_dp = lax.axis_size("dp")
    groups_expert = lax.axis_size("expert")
    group_size = groups_dp * groups_expert
    local_experts = w_gate.shape[1]
    experts_total = local_experts * group_size
    capacity = (9 * tokens * top_count + 8 * experts_total - 1) // (8 * experts_total)
    slot_total = experts_total * capacity
    norm_scale = norm_gain[0]
    normed_fwd = normalize(inputs, norm_scale)[0]
    normed_bwd, back_values, back_rms = normalize(bwd_inputs[0], norm_scale)
    fwd_slots = slot_of(fwd_routes[0], experts_total, capacity)
    bwd_slots = slot_of(bwd_routes[0], experts_total, capacity)
    packed_fwd = pack(normed_fwd, fwd_slots, slot_total, top_count)
    packed_bwd = pack(normed_bwd, bwd_slots, slot_total, top_count)
    packed_cot = pack(bwd_cotangent[0], bwd_slots, slot_total, top_count)
    arrived = (
        lax.all_to_all(packed_fwd, ("dp", "expert"), split_axis=0, concat_axis=0, tiled=True),
        lax.all_to_all(packed_bwd, ("dp", "expert"), split_axis=0, concat_axis=0, tiled=True),
        lax.all_to_all(packed_cot, ("dp", "expert"), split_axis=0, concat_axis=0, tiled=True),
    )
    block_shape = (group_size, local_experts, capacity, model_width)
    out_rows, d_rows = expert_work(
        arrived[0].reshape(block_shape),
        arrived[1].reshape(block_shape),
        arrived[2].reshape(block_shape),
        w_gate[0],
        w_up[0],
        w_down[0],
    )
    returned = (
        lax.all_to_all(
            out_rows.reshape(slot_total, model_width),
            ("dp", "expert"),
            split_axis=0,
            concat_axis=0,
            tiled=True,
        ),
        lax.all_to_all(
            d_rows.reshape(slot_total, model_width),
            ("dp", "expert"),
            split_axis=0,
            concat_axis=0,
            tiled=True,
        ),
    )
    fwd_back = returned[0][fwd_slots].reshape(tokens, top_count, model_width)
    bwd_back = returned[1][bwd_slots].reshape(tokens, top_count, model_width)
    combined = jnp.sum(fwd_back.astype(jnp.float32) * fwd_weights[0][:, :, None], axis=1)
    section_out = (inputs.astype(jnp.float32) + combined).astype(jnp.bfloat16)
    norm_grad = jnp.sum(bwd_back.astype(jnp.float32) * bwd_weights[0][:, :, None], axis=1)
    scaled = norm_scale * norm_grad
    section_grad = (
        bwd_cotangent[0].astype(jnp.float32)
        + back_rms * scaled
        - back_values * back_rms**3 * jnp.mean(back_values * scaled, axis=-1, keepdims=True)
    ).astype(jnp.bfloat16)
    next_forward = from_behind(section_out[None], "segment", 1)
    prev_grad = from_behind(section_grad[None], "segment", -1)
    return (next_forward, prev_grad)


def solution(mesh):
    placed = (
        P("segment", ("dp", "expert"), None),
        P("segment", ("dp", "expert"), None),
        P("segment", ("dp", "expert"), None),
        P("segment", ("dp", "expert"), None),
        P("segment", ("dp", "expert"), None),
        P("segment", ("dp", "expert"), None),
        P("segment", ("dp", "expert"), None),
        P("segment", None),
        P("segment", ("dp", "expert"), None, None),
        P("segment", ("dp", "expert"), None, None),
        P("segment", ("dp", "expert"), None, None),
    )
    return jax.shard_map(
        body,
        mesh=mesh,
        in_specs=placed,
        out_specs=(P("segment", ("dp", "expert"), None), P("segment", ("dp", "expert"), None)),
        check_vma=False,
    )
```

profile of v0, /device:TPU:9, one launch (start us, length us, event | category | flops | bytes accessed | tf_op | source)
XLA Modules:
  0.0 431.6 jit_solution(11154000519919316498)
XLA Ops:
  6.9 4.1 gather_fusion.2
  11.0 5.4 %all_to_all.39 = bf16[64,10,2048]{2,1,0:T(8,128)(2,1)} reshape(bf16[640,2048]{1,0:T(8,128)(2,1)} %gather_fusion.2) | data formatting | bytes 5242880 | tf_op jit(solution)/shard_map/all_to_all | solution.py:100
  16.3 9.9 %all-to-all-start.2 = ((bf16[64,10,2048]{2,1,0:T(8,128)(2,1)}), bf16[64,10,2048]{2,1,0:T(8,128)(2,1)}, u32[]{:S(2)}, u32[]{:S(2)}) async-start(bf16[64,10,2048]{2,1,0:T(8,128)(2,1)} %all_to_all.39), calls=%async_computation.2 | async-start | bytes 8388608 | tf_op jit(solution)/shard_map/all_to_all | solution.py:100
  26.6 4.2 gather_fusion.3
  30.7 5.4 %all_to_all.41 = bf16[64,10,2048]{2,1,0:T(8,128)(2,1)} reshape(bf16[640,2048]{1,0:T(8,128)(2,1)} %gather_fusion.3) | data formatting | bytes 5242880 | tf_op jit(solution)/shard_map/all_to_all | solution.py:99
  36.1 40.9 %all-to-all-done.2 = bf16[64,10,2048]{2,1,0:T(8,128)(2,1)} async-done(((bf16[64,10,2048]{2,1,0:T(8,128)(2,1)}), bf16[64,10,2048]{2,1,0:T(8,128)(2,1)}, u32[]{:S(2)}, u32[]{:S(2)}) %all-to-all-start.2) | async-done | bytes 2621472 | tf_op jit(solution)/shard_map/all_to_all | solution.py:100
  77.0 11.1 %all-to-all-start.3 = ((bf16[64,10,2048]{2,1,0:T(8,128)(2,1)}), bf16[64,10,2048]{2,1,0:T(8,128)(2,1)}, u32[]{:S(2)}, u32[]{:S(2)}) async-start(bf16[64,10,2048]{2,1,0:T(8,128)(2,1)} %all_to_all.41), calls=%async_computation.3 | async-start | bytes 8388608 | tf_op jit(solution)/shard_map/all_to_all | solution.py:99
  88.1 3.8 copy.33
  94.5 44.2 %all-to-all-done.3 = bf16[64,10,2048]{2,1,0:T(8,128)(2,1)} async-done(((bf16[64,10,2048]{2,1,0:T(8,128)(2,1)}), bf16[64,10,2048]{2,1,0:T(8,128)(2,1)}, u32[]{:S(2)}, u32[]{:S(2)}) %all-to-all-start.3) | async-done | bytes 2621472 | tf_op jit(solution)/shard_map/all_to_all | solution.py:99
  138.7 3.8 copy.34
  144.0 2.6 fusion.40
  146.6 8.5 %fusion.2 = f32[2,64,5,2048]{3,1,2,0:T(8,128)} fusion(bf16[1,2,2048,384]{3,2,1,0:T(8,128)(2,1)} %param.19, f32[64,2,5,384]{3,0,2,1:T(8,128)} %fusion.16, bf16[64,2,5,2048]{3,0,2,1:T(8,128)(2,1)} %bitcast.174, bf16[1,2,2048,384]{3,2,1,0:T(8,128)(2,1)S(1)} %copy-done, f32[64,2,5,384]{3,0,2,1:T(8,128)} %fusion.40), kind=kOutput, calls=%fused_computation.13 | convolution fusion | flops 2015723520 | bytes 16121856 | tf_op jit(solution)/shard_map/gecf,edf->gecd/dot_general | solution.py:59
  155.1 4.7 %add_convert_fusion = bf16[2,64,5,2048]{3,1,2,0:T(8,128)(2,1)S(1)} fusion(f32[2,64,5,2048]{3,1,2,0:T(8,128)} %fusion.2, bf16[1,2,2048,384]{3,2,1,0:T(8,128)(2,1)S(1)} %copy-done, f32[64,2,5,384]{3,0,2,1:T(8,128)} %fusion.16, f32[64,2,5,384]{3,0,2,1:T(8,128)} %fusion.40), kind=kOutput, calls=%fused_computation.7 | convolution fusion | flops 1010728960 | bytes 12976128 | tf_op jit(solution)/shard_map/gecf,edf->gecd/dot_general | solution.py:60
  159.7 3.6 copy.35
  163.3 11.4 %all-to-all-start.4 = ((bf16[64,10,2048]{2,1,0:T(8,128)(2,1)}), bf16[64,10,2048]{2,1,0:T(8,128)(2,1)}, u32[]{:S(2)}, u32[]{:S(2)}) async-start(bf16[64,10,2048]{2,1,0:T(8,128)(2,1)} %copy.35), calls=%async_computation.4 | async-start | bytes 8388608 | tf_op jit(solution)/shard_map/all_to_all | solution.py:119
  180.2 45.0 %all-to-all-done.4 = bf16[64,10,2048]{2,1,0:T(8,128)(2,1)} async-done(((bf16[64,10,2048]{2,1,0:T(8,128)(2,1)}), bf16[64,10,2048]{2,1,0:T(8,128)(2,1)}, u32[]{:S(2)}, u32[]{:S(2)}) %all-to-all-start.4) | async-done | bytes 2621472 | tf_op jit(solution)/shard_map/all_to_all | solution.py:119
  225.2 5.5 %all_to_all.45 = bf16[640,2048]{1,0:T(8,128)(2,1)} reshape(bf16[64,10,2048]{2,1,0:T(8,128)(2,1)} %all-to-all-done.4) | data formatting | bytes 5242880 | tf_op jit(solution)/shard_map/all_to_all | solution.py:119
  230.8 7.4 %gather_fusion.4 = bf16[512,2048]{1,0:T(8,128)(2,1)} fusion(bf16[640,2048]{1,0:T(8,128)(2,1)} %all_to_all.45, s32[1024]{0:T(1024)S(1)} %pad_clamp_fusion), kind=kCustom, calls=%fused_computation.4 | custom fusion | bytes 4196352 | tf_op jit(solution)/shard_map/gather | solution.py:128
  238.2 3.4 fusion
  243.1 4.1 gather_fusion
  247.2 5.4 %all_to_all.34 = bf16[64,10,2048]{2,1,0:T(8,128)(2,1)} reshape(bf16[640,2048]{1,0:T(8,128)(2,1)} %gather_fusion) | data formatting | bytes 5242880 | tf_op jit(solution)/shard_map/all_to_all | solution.py:98
  252.5 60.2 %all_to_all.51 = bf16[64,10,2048]{2,1,0:T(8,128)(2,1)S(1)} all-to-all(bf16[64,10,2048]{2,1,0:T(8,128)(2,1)} %all_to_all.34), channel_id=1, replica_groups=mesh['segment'=4,'dp'=4,'expert'=16] {'dp','expert'}, dimensions={0} | all-to-all | bytes 5242880 | tf_op jit(solution)/shard_map/all_to_all | solution.py:98
  318.2 7.4 %convolution_convert_fusion = bf16[2,64,5,2048]{3,1,2,0:T(8,128)(2,1)} fusion(bf16[1,2,384,2048]{3,2,1,0:T(8,128)(2,1)} %param.21, bf16[64,2,5,2048]{3,0,2,1:T(8,128)(2,1)} %bitcast.176, bf16[1,2,2048,384]{3,2,1,0:T(8,128)(2,1)S(1)} %copy-done, f32[64,2,5,384]{3,0,2,1:T(8,128)} %fusion.37), kind=kOutput, calls=%fused_computation.12 | convolution fusion | flops 2016051200 | bytes 12517376 | tf_op jit(solution)/shard_map/gecf,efd->gecd/dot_general | solution.py:43
  325.6 5.3 %copy.26 = bf16[64,10,2048]{2,1,0:T(8,128)(2,1)} copy(bf16[64,10,2048]{2,0,1:T(8,128)(2,1)} %bitcast.177) | data formatting | bytes 5242880 | tf_op jit(solution)/shard_map/all_to_all | solution.py:112
  330.9 8.6 %all-to-all-start.1 = ((bf16[64,10,2048]{2,1,0:T(8,128)(2,1)}), bf16[64,10,2048]{2,1,0:T(8,128)(2,1)}, u32[]{:S(2)}, u32[]{:S(2)}) async-start(bf16[64,10,2048]{2,1,0:T(8,128)(2,1)} %copy.26), calls=%async_computation.1 | async-start | bytes 8388608 | tf_op jit(solution)/shard_map/all_to_all | solution.py:112
  341.7 5.3 %collective-permute-start.1 = (bf16[1,64,2048]{2,1,0:T(8,128)(2,1)}, bf16[1,64,2048]{2,1,0:T(8,128)(2,1)}, u32[]{:S(2)}, u32[]{:S(2)}) collective-permute-start(bf16[1,64,2048]{2,1,0:T(8,128)(2,1)} %fusion.68), channel_id=1, source_target_pairs={{0,192},{64,0},{128,64},{192,128},{1,193},{65,1},{129,65},{193,129... | collective-permute-start | bytes 786440 | tf_op jit(solution)/shard_map/ppermute | solution.py:12
  347.1 48.7 %all-to-all-done.1 = bf16[64,10,2048]{2,1,0:T(8,128)(2,1)} async-done(((bf16[64,10,2048]{2,1,0:T(8,128)(2,1)}), bf16[64,10,2048]{2,1,0:T(8,128)(2,1)}, u32[]{:S(2)}, u32[]{:S(2)}) %all-to-all-start.1) | async-done | bytes 2621472 | tf_op jit(solution)/shard_map/all_to_all | solution.py:112
  395.7 5.5 %all_to_all.38 = bf16[640,2048]{1,0:T(8,128)(2,1)} reshape(bf16[64,10,2048]{2,1,0:T(8,128)(2,1)} %all-to-all-done.1) | data formatting | bytes 5242880 | tf_op jit(solution)/shard_map/all_to_all | solution.py:112
  401.3 7.4 %gather_fusion.1 = bf16[512,2048]{1,0:T(8,128)(2,1)} fusion(bf16[640,2048]{1,0:T(8,128)(2,1)} %all_to_all.38, s32[1024]{0:T(1024)S(1)} %pad_clamp_fusion.2), kind=kCustom, calls=%fused_computation.1 | custom fusion | bytes 4196352 | tf_op jit(solution)/shard_map/gather | solution.py:127
  408.7 3.4 fusion.1
  412.2 3.2 collective-permute-start
  415.4 13.6 %collective-permute-done = bf16[1,64,2048]{2,1,0:T(8,128)(2,1)S(1)} collective-permute-done((bf16[1,64,2048]{2,1,0:T(8,128)(2,1)S(1)}, bf16[1,64,2048]{2,1,0:T(8,128)(2,1)S(1)}, u32[]{:S(2)}, u32[]{:S(2)}) %collective-permute-start) | collective-permute-done | bytes 262176 | tf_op jit(solution)/shard_map/ppermute | solution.py:12
  (95 shorter events, 27.5 us)
Async XLA Ops:
  0.6 145.9 %copy-start = (bf16[1,2,2048,384]{3,2,1,0:T(8,128)(2,1)S(1)}, bf16[1,2,2048,384]{3,2,1,0:T(8,128)(2,1)}, u32[]{:S(2)}) copy-start(bf16[1,2,2048,384]{3,2,1,0:T(8,128)(2,1)} %param.20) | copy-start | bytes 9437188
  16.3 9.9 %copy-start.2 = (bf16[1,64,2048]{2,1,0:T(8,128)(2,1)S(1)}, bf16[1,64,2048]{2,1,0:T(8,128)(2,1)}, u32[]{:S(2)}) copy-start(bf16[1,64,2048]{2,1,0:T(8,128)(2,1)} %param.14) | copy-start | bytes 786436
  16.3 10.1 %copy-start.10 = (f32[1,2048]{1,0:T(1,128)S(1)}, f32[1,2048]{1,0:T(1,128)}, u32[]{:S(2)}) copy-start(f32[1,2048]{1,0:T(1,128)} %param.18) | copy-start | bytes 24580
  16.3 60.7 %all-to-all-start.2 = ((bf16[64,10,2048]{2,1,0:T(8,128)(2,1)}), bf16[64,10,2048]{2,1,0:T(8,128)(2,1)}, u32[]{:S(2)}, u32[]{:S(2)}) async-start(bf16[64,10,2048]{2,1,0:T(8,128)(2,1)} %all_to_all.39), calls=%async_computation.2 | async-start | bytes 8388608 | tf_op jit(solution)/shard_map/all_to_all | solution.py:100
  77.0 61.7 %all-to-all-start.3 = ((bf16[64,10,2048]{2,1,0:T(8,128)(2,1)}), bf16[64,10,2048]{2,1,0:T(8,128)(2,1)}, u32[]{:S(2)}, u32[]{:S(2)}) async-start(bf16[64,10,2048]{2,1,0:T(8,128)(2,1)} %all_to_all.41), calls=%async_computation.3 | async-start | bytes 8388608 | tf_op jit(solution)/shard_map/all_to_all | solution.py:99
  88.1 3.8 copy-start.16
  138.7 5.3 %copy-start.14 = (bf16[1,2,2048,384]{3,2,1,0:T(8,128)(2,1)S(1)}, bf16[1,2,2048,384]{3,2,1,0:T(8,128)(2,1)}, u32[]{:S(2)}) copy-start(bf16[1,2,2048,384]{3,2,1,0:T(8,128)(2,1)} %param.19) | copy-start | bytes 9437188
  142.5 1.5 copy-start.5
  163.3 11.4 %copy-start.11 = (s32[1,64,8]{1,2,0:T(8,128)S(1)}, s32[1,64,8]{1,2,0:T(8,128)}, u32[]{:S(2)}) copy-start(s32[1,64,8]{1,2,0:T(8,128)} %param.12) | copy-start | bytes 6148
  163.3 11.7 %copy-start.12 = (f32[1,64,8]{1,2,0:T(8,128)S(1)}, f32[1,64,8]{1,2,0:T(8,128)}, u32[]{:S(2)}) copy-start(f32[1,64,8]{1,2,0:T(8,128)} %param.17) | copy-start | bytes 6148
  163.3 16.7 %copy-start.7 = (bf16[1,64,2048]{2,1,0:T(8,128)(2,1)S(1)}, bf16[1,64,2048]{2,1,0:T(8,128)(2,1)}, u32[]{:S(2)}) copy-start(bf16[1,64,2048]{2,1,0:T(8,128)(2,1)} %param.11) | copy-start | bytes 786436
  163.3 61.9 %all-to-all-start.4 = ((bf16[64,10,2048]{2,1,0:T(8,128)(2,1)}), bf16[64,10,2048]{2,1,0:T(8,128)(2,1)}, u32[]{:S(2)}, u32[]{:S(2)}) async-start(bf16[64,10,2048]{2,1,0:T(8,128)(2,1)} %copy.35), calls=%async_computation.4 | async-start | bytes 8388608 | tf_op jit(solution)/shard_map/all_to_all | solution.py:119
  175.6 0.7 copy-start.9
  230.8 10.9 %copy-start.3 = (bf16[1,64,2048]{2,1,0:T(8,128)(2,1)S(1)}, bf16[1,64,2048]{2,1,0:T(8,128)(2,1)}, u32[]{:S(2)}) copy-start(bf16[1,64,2048]{2,1,0:T(8,128)(2,1)} %param.14) | copy-start | bytes 786436
  241.6 1.4 copy-start.1
  312.7 3.0 copy-start.15
  314.2 1.5 copy-start.6
  330.9 8.6 %copy-start.13 = (f32[1,64,8]{1,2,0:T(8,128)S(1)}, f32[1,64,8]{1,2,0:T(8,128)}, u32[]{:S(2)}) copy-start(f32[1,64,8]{1,2,0:T(8,128)} %param.13) | copy-start | bytes 6148
  330.9 8.7 %copy-start.4 = (bf16[1,64,2048]{2,1,0:T(8,128)(2,1)S(1)}, bf16[1,64,2048]{2,1,0:T(8,128)(2,1)}, u32[]{:S(2)}) copy-start(bf16[1,64,2048]{2,1,0:T(8,128)(2,1)} %param.14) | copy-start | bytes 786436
  330.9 64.8 %all-to-all-start.1 = ((bf16[64,10,2048]{2,1,0:T(8,128)(2,1)}), bf16[64,10,2048]{2,1,0:T(8,128)(2,1)}, u32[]{:S(2)}, u32[]{:S(2)}) async-start(bf16[64,10,2048]{2,1,0:T(8,128)(2,1)} %copy.26), calls=%async_computation.1 | async-start | bytes 8388608 | tf_op jit(solution)/shard_map/all_to_all | solution.py:112
  341.7 73.7 %collective-permute-start.1 = (bf16[1,64,2048]{2,1,0:T(8,128)(2,1)}, bf16[1,64,2048]{2,1,0:T(8,128)(2,1)}, u32[]{:S(2)}, u32[]{:S(2)}) collective-permute-start(bf16[1,64,2048]{2,1,0:T(8,128)(2,1)} %fusion.68), channel_id=1, source_target_pairs={{0,192},{64,0},{128,64},{192,128},{1,193},{65,1},{129,65},{193,129... | collective-permute-start | bytes 786440 | tf_op jit(solution)/shard_map/ppermute | solution.py:12
  401.3 10.9 %copy-start.8 = (bf16[1,64,2048]{2,1,0:T(8,128)(2,1)S(1)}, bf16[1,64,2048]{2,1,0:T(8,128)(2,1)}, u32[]{:S(2)}) copy-start(bf16[1,64,2048]{2,1,0:T(8,128)(2,1)} %param.11) | copy-start | bytes 786436
  412.2 16.8 %collective-permute-start = (bf16[1,64,2048]{2,1,0:T(8,128)(2,1)S(1)}, bf16[1,64,2048]{2,1,0:T(8,128)(2,1)S(1)}, u32[]{:S(2)}, u32[]{:S(2)}) collective-permute-start(bf16[1,64,2048]{2,1,0:T(8,128)(2,1)S(1)} %fusion.61), channel_id=1, source_target_pairs={{0,64},{64,128},{128,192},{192,0},{1,65},{65,129},{129,193},{193,1... | collective-permute-start | bytes 786440 | tf_op jit(solution)/shard_map/ppermute | solution.py:12
where the time goes:
time: 438 us; the launch traced here: 432 us
  waiting for transfers between devices  192 us (44%)
  local copies, waits for them, and re-layouts  86.4 us (20%)
  blocking collectives  60.2 us (14%)
  starting transfers between devices  49.5 us (11%)
  matrix products  28.2 us (6%)
  other arithmetic  13.7 us (3%)
    all_to_all x1, blocking collectives, body(): lax.all_to_all(packed_fwd, ('dp', 'expert'), split_axis=0, concat_axis=0,...  60.2 us
    all_to_all x1, waiting for transfers between devices, body(): lax.all_to_all(out_rows.reshape(slot_total, model_width), ('dp', 'expert'...  48.7 us
    all_to_all x1, waiting for transfers between devices, body(): lax.all_to_all(d_rows.reshape(slot_total, model_width), ('dp', 'expert'),...  45 us
    all_to_all x1, waiting for transfers between devices, body(): lax.all_to_all(packed_bwd, ('dp', 'expert'), split_axis=0, concat_axis=0,...  44.2 us
    all_to_all x1, waiting for transfers between devices, body(): lax.all_to_all(packed_cot, ('dp', 'expert'), split_axis=0, concat_axis=0,...  40.9 us
    ppermute x2, waiting for transfers between devices, from_behind(): return lax.ppermute(value, axis, pairs)  13.6 us
    gather x3, local copies, waits for them, and re-layouts, pack(): return padded[owners]  12.3 us
    all_to_all x1, starting transfers between devices, body(): lax.all_to_all(d_rows.reshape(slot_total, model_width), ('dp', 'expert'),...  11.4 us
  transfers between devices with their start and end apart: 6, of which 5 were waited for; matrix products, arithmetic and copies ran while one was open for 7% of the time, Pallas kernels for 0%

commit v1 on v0

v1 whole, which is shorter than its diff:
```python
import jax
import jax.numpy as jnp
from jax import lax
from jax.experimental import pallas as pl
from jax.experimental.pallas import tpu as pltpu
from jax.sharding import PartitionSpec as P

EPSILON = 1e-06
BF = jnp.bfloat16
F32 = jnp.float32
SLOTS = 5
ROWS = 4
NN = (((1,), (0,)), ((), ()))
NT = (((1,), (1,)), ((), ()))


def dot(left, right, dims=NN):
    return lax.dot_general(left, right, dims, preferred_element_type=F32)


def iota(shape, axis):
    return lax.broadcasted_iota(jnp.int32, shape, axis)


def onehot(mask):
    return jnp.where(mask, 1.0, 0.0).astype(BF)


def slot_marks(routes, experts):
    tokens, top = routes.shape
    lanes = iota((tokens, experts), 1)
    member = jnp.zeros((tokens, experts), F32)
    for k in range(top):
        member = jnp.where(routes[:, k : k + 1] == lanes, 1.0, member)
    upto = onehot(iota((tokens, tokens), 1) <= iota((tokens, tokens), 0))
    return (dot(upto, member.astype(BF)) * member).astype(BF)


def normalize(inputs, norm_scale):
    values = inputs.astype(F32)
    inv_rms = lax.rsqrt(jnp.mean(values * values, axis=-1, keepdims=True) + EPSILON)
    return values * inv_rms * norm_scale, values, inv_rms


def pack_kernel(experts, fwd, bwd, cot, fwd_routes, bwd_routes, gain, out, tile, sems):
    tokens, width = fwd.shape
    quarter = width // ROWS
    wide = width + quarter
    rows = experts * ROWS
    copies = []

    def masks(routes):
        marks = slot_marks(routes[...], experts)
        spread = onehot(iota((rows, experts), 0) // ROWS == iota((rows, experts), 1))
        table = dot(spread, jnp.concatenate([marks] * ROWS, axis=0), NT)
        place = iota((rows, ROWS * tokens), 0) % ROWS
        last = onehot((table == SLOTS) & (place == iota((rows, ROWS * tokens), 1) // tokens))
        main = onehot(table[:, :tokens] == (place[:, :tokens] + 1).astype(F32))
        return main, last

    def emit(index, values, main, last):
        for q in range(ROWS):
            cols = pl.ds(q * quarter, quarter)
            tile[index, :, cols] = dot(main, values[:, q * quarter : (q + 1) * quarter]).astype(BF)
        stacked = jnp.concatenate(
            [values[:, q * quarter : (q + 1) * quarter] for q in range(ROWS)], axis=0
        )
        tile[index, :, pl.ds(width, quarter)] = dot(last, stacked).astype(BF)
        copy = pltpu.make_async_copy(
            tile.at[index], out.at[:, pl.ds(index * wide, wide)], sems.at[index]
        )
        copy.start()
        copies.append(copy)

    main, last = masks(bwd_routes)
    emit(2, cot[...], main, last)
    emit(1, normalize(bwd[...], gain[...])[0].astype(BF), main, last)
    main, last = masks(fwd_routes)
    emit(0, normalize(fwd[...], gain[...])[0].astype(BF), main, last)
    for copy in copies:
        copy.wait()


def expert_kernel(
    arrived, w_gate, w_up, w_down, out, got, gate, up, down, rows_in, outs, lasts, back, sems
):
    local, width, hidden = w_gate.shape
    quarter = width // ROWS
    wide = width + quarter
    total = arrived.shape[0]
    span = local * ROWS
    groups = total // span
    bulk = groups * ROWS
    loads = []
    for a in range(3):
        loads.append(
            pltpu.make_async_copy(arrived.at[:, pl.ds(a * wide, wide)], got.at[a], sems.at[a])
        )
    loads.append(pltpu.make_async_copy(w_gate, gate, sems.at[3]))
    loads.append(pltpu.make_async_copy(w_up, up, sems.at[4]))
    loads.append(pltpu.make_async_copy(w_down, down, sems.at[5]))
    for load in loads:
        load.start()

    def per_array(a):
        def per_expert(e, carry):
            m = iota((bulk, total), 0)
            pick = onehot(iota((bulk, total), 1) == (m // ROWS) * span + e * ROWS + m % ROWS)
            tail = onehot(iota((bulk, total), 1) == (m % groups) * span + e * ROWS + m // groups)

            for q in range(ROWS):
                cols = pl.ds(q * quarter, quarter)
                rows_in[a, e, pl.ds(0, bulk), cols] = dot(pick, got[a, :, cols]).astype(BF)
            rest = dot(tail, got[a, :, pl.ds(width, quarter)]).astype(BF)
            for q in range(ROWS):
                rows_in[a, e, pl.ds(bulk, groups), pl.ds(q * quarter, quarter)] = rest[
                    q * groups : (q + 1) * groups
                ]
            return carry

        lax.fori_loop(0, local, per_expert, 0)

    def put(b, e, q, values):
        values = values.astype(BF)
        cols = pl.ds(q * quarter, quarter)
        outs[b, pl.ds(e * bulk, bulk), cols] = values[:bulk]
        lasts[b, pl.ds((e * ROWS + q) * groups, groups), :] = values[bulk:]

    def finish(b):
        side = local * bulk
        i = iota((total, side), 0)
        c = iota((total, side), 1)
        m = c % bulk
        spread = onehot(i == (m // ROWS) * span + (c // bulk) * ROWS + m % ROWS)
        tail = onehot(i == (c % groups) * span + c // groups)
        for q in range(ROWS):
            cols = pl.ds(q * quarter, quarter)
            back[b, :, cols] = dot(spread, outs[b, :, cols]).astype(BF)
        back[b, :, pl.ds(width, quarter)] = dot(tail, lasts[b]).astype(BF)
        copy = pltpu.make_async_copy(
            back.at[b], out.at[:, pl.ds(b * wide, wide)], sems.at[6 + b]
        )
        copy.start()
        return copy

    def forward(e, carry):
        x = rows_in[0, e]
        g = dot(x, gate[e])
        u = dot(x, up[e])
        act = (g * jax.nn.sigmoid(g) * u).astype(BF)
        for q in range(ROWS):
            put(0, e, q, dot(act, down[e, :, pl.ds(q * quarter, quarter)]))
        return carry

    def backward(e, carry):
        x = rows_in[1, e]
        g = dot(x, gate[e])
        u = dot(x, up[e])
        h = dot(rows_in[2, e], down[e], NT)
        s = jax.nn.sigmoid(g)
        d_gate = (h * u * s * (1.0 + g * (1.0 - s))).astype(BF)
        d_up = (h * g * s).astype(BF)
        for q in range(ROWS):
            part = pl.ds(q * quarter, quarter)
            put(1, e, q, dot(d_gate, gate[e, part, :], NT) + dot(d_up, up[e, part, :], NT))
        return carry

    loads[0].wait()
    per_array(0)
    for load in loads[3:]:
        load.wait()
    lax.fori_loop(0, local, forward, 0)
    first = finish(0)
    loads[1].wait()
    per_array(1)
    loads[2].wait()
    per_array(2)
    lax.fori_loop(0, local, backward, 0)
    second = finish(1)
    first.wait()
    second.wait()


def weighted_sum(experts, returned, routes, weights):
    tokens, top = routes.shape
    wide = returned.shape[1]
    quarter = wide // (ROWS + 1)
    width = quarter * ROWS
    rows = experts * ROWS
    marks = slot_marks(routes, experts)
    spread = onehot(iota((rows, experts), 0) // ROWS == iota((rows, experts), 1))
    table = dot(marks, spread, NT)
    column = iota((tokens, rows), 1)
    factor = jnp.zeros((tokens, rows), F32)
    for k in range(top):
        factor = jnp.where(routes[:, k : k + 1] == column // ROWS, weights[:, k : k + 1], factor)
    place = column % ROWS

    def split(values):
        high = values.astype(BF)
        return high, (values - high.astype(F32)).astype(BF)

    main = jnp.concatenate(
        split(jnp.where(table == (place + 1).astype(F32), factor, 0.0)), axis=0
    )
    tails = []
    for q in range(ROWS):
        tails.extend(split(jnp.where((table == SLOTS) & (place == q), factor, 0.0)))
    extra = dot(jnp.concatenate(tails, axis=0), returned[:, pl.ds(width, quarter)])
    pieces = []
    for q in range(ROWS):
        piece = dot(main, returned[:, pl.ds(q * quarter, quarter)])
        at = 2 * q * tokens
        pieces.append(
            (piece[:tokens] + piece[tokens:])
            + (extra[at : at + tokens] + extra[at + tokens : at + 2 * tokens])
        )
    return jnp.concatenate(pieces, axis=1)


def forward_kernel(experts, returned, inputs, routes, weights, out):
    combined = weighted_sum(experts, returned, routes[...], weights[...])
    out[...] = (inputs[...].astype(F32) + combined).astype(BF)


def backward_kernel(experts, returned, inputs, cot, routes, weights, gain, out):
    norm_grad = weighted_sum(experts, returned, routes[...], weights[...])
    norm_scale = gain[...]
    _, values, inv_rms = normalize(inputs[...], norm_scale)
    scaled = norm_scale * norm_grad
    mean = jnp.mean(values * scaled, axis=-1, keepdims=True)
    out[...] = (
        cot[...].astype(F32) + inv_rms * scaled - values * (inv_rms * inv_rms * inv_rms) * mean
    ).astype(BF)


def from_behind(value, axis, steps):
    count = lax.axis_size(axis)
    pairs = [(source, (source + steps) % count) for source in range(count)]
    return lax.ppermute(value, axis, pairs)


def body(
    fwd_inputs,
    fwd_routes,
    fwd_weights,
    bwd_inputs,
    bwd_cotangent,
    bwd_routes,
    bwd_weights,
    norm_gain,
    w_gate,
    w_up,
    w_down,
):
    _, tokens, width = fwd_inputs.shape
    local = w_gate.shape[1]
    hidden = w_gate.shape[3]
    group = lax.axis_size("dp") * lax.axis_size("expert")
    experts = local * group
    rows = experts * ROWS
    quarter = width // ROWS
    wide = width + quarter
    bulk = group * ROWS
    vmem = pl.BlockSpec(memory_space=pltpu.VMEM)
    hbm = pl.BlockSpec(memory_space=pl.ANY)
    limit = pltpu.CompilerParams(vmem_limit_bytes=60 * 1024 * 1024)

    packed = pl.pallas_call(
        lambda *refs: pack_kernel(experts, *refs),
        out_shape=jax.ShapeDtypeStruct((rows, 3 * wide), BF),
        in_specs=[vmem] * 6,
        out_specs=hbm,
        scratch_shapes=[pltpu.VMEM((3, rows, wide), BF), pltpu.SemaphoreType.DMA((3,))],
        compiler_params=limit,
        name="pack",
    )(fwd_inputs[0], bwd_inputs[0], bwd_cotangent[0], fwd_routes[0], bwd_routes[0], norm_gain)

    arrived = lax.all_to_all(packed, ("dp", "expert"), split_axis=0, concat_axis=0, tiled=True)

    worked = pl.pallas_call(
        expert_kernel,
        out_shape=jax.ShapeDtypeStruct((rows, 2 * wide), BF),
        in_specs=[hbm] * 4,
        out_specs=hbm,
        scratch_shapes=[
            pltpu.VMEM((3, rows, wide), BF),
            pltpu.VMEM((local, width, hidden), BF),
            pltpu.VMEM((local, width, hidden), BF),
            pltpu.VMEM((local, hidden, width), BF),
            pltpu.VMEM((3, local, bulk + group, width), BF),
            pltpu.VMEM((2, local * bulk, width), BF),
            pltpu.VMEM((2, local * ROWS * group, quarter), BF),
            pltpu.VMEM((2, rows, wide), BF),
            pltpu.SemaphoreType.DMA((8,)),
        ],
        compiler_params=limit,
        name="experts",
    )(arrived, w_gate[0], w_up[0], w_down[0])

    returned = lax.all_to_all(worked, ("dp", "expert"), split_axis=0, concat_axis=0, tiled=True)

    def whole(array):
        return pl.BlockSpec(array.shape, lambda i: (0,) * array.ndim)

    def combine(kernel, part, *rest, name):
        return pl.pallas_call(
            lambda *refs: kernel(experts, *refs),
            out_shape=jax.ShapeDtypeStruct((tokens, width), BF),
            grid=(1,),
            in_specs=[pl.BlockSpec((rows, wide), lambda i: (0, part))] + [whole(r) for r in rest],
            out_specs=pl.BlockSpec((tokens, width), lambda i: (0, 0)),
            compiler_params=limit,
            name=name,
        )(returned, *rest)

    section_out = combine(
        forward_kernel, 0, fwd_inputs[0], fwd_routes[0], fwd_weights[0], name="forward"
    )
    section_grad = combine(
        backward_kernel,
        1,
        bwd_inputs[0],
        bwd_cotangent[0],
        bwd_routes[0],
        bwd_weights[0],
        norm_gain,
        name="backward",
    )
    next_forward = from_behind(section_out[None], "segment", 1)
    prev_grad = from_behind(section_grad[None], "segment", -1)
    return (next_forward, prev_grad)


def solution(mesh):
    token = P("segment", ("dp", "expert"), None)
    weight = P("segment", ("dp", "expert"), None, None)
    return jax.shard_map(
        body,
        mesh=mesh,
        in_specs=(token,) * 7 + (P("segment", None),) + (weight,) * 3,
        out_specs=(token, token),
        check_vma=False,
    )
```

time: 438 us -> 238 us (0.54)
  the two profiles are of different devices: /device:TPU:9 before, /device:TPU:32 now
where the time goes in v1:
time: 238 us; the launch traced here: 237 us
  blocking collectives  99.1 us (42%)
  waiting for transfers between devices  79.1 us (33%)
  Pallas kernels  39.1 us (16%)
  starting transfers between devices  13.7 us (6%)
  local copies, waits for them, and re-layouts  5.54 us (2%)
    all_to_all x1, blocking collectives, body(): lax.all_to_all(packed, ('dp', 'expert'), split_axis=0, concat_axis=0, til...  99.1 us
    all_to_all x1, waiting for transfers between devices, body(): lax.all_to_all(worked, ('dp', 'expert'), split_axis=0, concat_axis=0, til...  62.6 us
    pallas_call x1, Pallas kernels, body(): pl.pallas_call(expert_kernel, out_shape=jax.ShapeDtypeStruct((rows, 2 * w...  25.9 us
    ppermute x2, waiting for transfers between devices, from_behind(): return lax.ppermute(value, axis, pairs)  16.4 us
    all_to_all x1, starting transfers between devices, body(): lax.all_to_all(worked, ('dp', 'expert'), split_axis=0, concat_axis=0, til...  8.28 us
    pallas_call x2, Pallas kernels, combine(): pl.pallas_call(lambda *refs: kernel(experts, *refs), out_shape=jax.ShapeD...  7.48 us
    pallas_call x1, Pallas kernels, body(): pl.pallas_call(lambda *refs: pack_kernel(experts, *refs), out_shape=jax.S...  5.8 us
    unnamed x10, local copies, waits for them, and re-layouts  5.54 us
  transfers between devices with their start and end apart: 3, of which 3 were waited for; matrix products, arithmetic and copies ran while one was open for 1% of the time, Pallas kernels for 2%

profile of v1, /device:TPU:32, one launch (start us, length us, event | category | flops | bytes accessed | tf_op | source)
XLA Modules:
  0.0 237.2 jit_solution(6211449506153257160)
XLA Ops:
  0.6 1.4 copy.13
  2.0 1.4 copy.14
  3.4 5.8 %pack.1 = bf16[512,7680]{1,0:T(8,128)(2,1)} custom-call(bf16[64,2048]{1,0:T(8,128)(2,1)} %bitcast.26, bf16[64,2048]{1,0:T(8,128)(2,1)} %bitcast.22, bf16[64,2048]{1,0:T(8,128)(2,1)} %bitcast.24, s32[64,8]{1,0:T(8,128)} %bitcast.28, s32[64,8]{1,0:T(8,128)} %bitcast.30, f32[1,2048]{1,0:T(1,128)} %refs_5_.3), custom_call_target="tpu_custom_call" | custom-call | tf_op jit(solution)/shard_map/pack/pallas_call | solution.py:269
  9.2 99.1 %all_to_all.22 = bf16[64,8,7680]{2,1,0:T(8,128)(2,1)} all-to-all(bf16[64,8,7680]{2,1,0:T(8,128)(2,1)} %bitcast.16), channel_id=1, replica_groups=mesh['segment'=4,'dp'=4,'expert'=16] {'dp','expert'}, dimensions={0} | all-to-all | bytes 15728640 | tf_op jit(solution)/shard_map/all_to_all | solution.py:279
  108.3 25.9 %experts.1 = bf16[512,5120]{1,0:T(8,128)(2,1)} custom-call(bf16[512,7680]{1,0:T(8,128)(2,1)} %bitcast.17, bf16[2,2048,384]{2,1,0:T(8,128)(2,1)} %bitcast.19, bf16[2,2048,384]{2,1,0:T(8,128)(2,1)} %bitcast.20, bf16[2,384,2048]{2,1,0:T(8,128)(2,1)} %bitcast.21), custom_call_target="tpu_custom_call" | custom-call | tf_op jit(solution)/shard_map/experts/pallas_call | solution.py:281
  134.2 0.0 copy-start
  134.2 0.0 copy-start.1
  134.2 8.3 %all-to-all-start.1 = ((bf16[64,8,5120]{2,1,0:T(8,128)(2,1)}), bf16[64,8,5120]{2,1,0:T(8,128)(2,1)}, u32[]{:S(2)}, u32[]{:S(2)}) async-start(bf16[64,8,5120]{2,1,0:T(8,128)(2,1)} %bitcast.18), calls=%async_computation.1 | async-start | bytes 10485760 | tf_op jit(solution)/shard_map/all_to_all | solution.py:301
  142.5 0.0 copy-done
  142.5 0.7 copy.16
  143.2 0.0 copy-done.1
  143.2 0.7 copy.15
  143.9 62.6 %all-to-all-done.1 = bf16[64,8,5120]{2,1,0:T(8,128)(2,1)} async-done(((bf16[64,8,5120]{2,1,0:T(8,128)(2,1)}), bf16[64,8,5120]{2,1,0:T(8,128)(2,1)}, u32[]{:S(2)}, u32[]{:S(2)}) %all-to-all-start.1) | async-done | bytes 5242912 | tf_op jit(solution)/shard_map/all_to_all | solution.py:301
  206.5 3.8 %backward.1 = bf16[64,2048]{1,0:T(8,128)(2,1)} custom-call(bf16[512,5120]{1,0:T(8,128)(2,1)} %bitcast.11.refs_0_, bf16[64,2048]{1,0:T(8,128)(2,1)} %bitcast.23, bf16[64,2048]{1,0:T(8,128)(2,1)} %bitcast.25, s32[64,8]{1,0:T(8,128)} %bitcast.31, f32[64,8]{1,0:T(8,128)} %bitcast.35, f32[1,2048]{1,0:T(1,128)} %refs_5_.3), custom_call_target="tpu_custom_call" | custom-call | tf_op jit(solution)/shard_map/backward/pallas_call | solution.py:307
  210.4 5.4 %collective-permute-start.1 = (bf16[1,64,2048]{2,1,0:T(8,128)(2,1)}, bf16[1,64,2048]{2,1,0:T(8,128)(2,1)S(1)}, u32[]{:S(2)}, u32[]{:S(2)}) collective-permute-start(bf16[1,64,2048]{2,1,0:T(8,128)(2,1)} %bitcast.32), channel_id=1, source_target_pairs={{0,192},{64,0},{128,64},{192,128},{1,193},{65,1},{129,65},{193,129... | collective-permute-start | bytes 786440 | tf_op jit(solution)/shard_map/ppermute | solution.py:240
  215.8 3.7 %forward.1 = bf16[64,2048]{1,0:T(8,128)(2,1)} custom-call(bf16[512,5120]{1,0:T(8,128)(2,1)} %bitcast.11.refs_0_, bf16[64,2048]{1,0:T(8,128)(2,1)} %bitcast.27, s32[64,8]{1,0:T(8,128)} %bitcast.29, f32[64,8]{1,0:T(8,128)} %bitcast.34), custom_call_target="tpu_custom_call" | custom-call | tf_op jit(solution)/shard_map/forward/pallas_call | solution.py:307
  219.4 0.0 collective-permute-start
  219.4 8.3 %collective-permute-done.1 = bf16[1,64,2048]{2,1,0:T(8,128)(2,1)S(1)} collective-permute-done((bf16[1,64,2048]{2,1,0:T(8,128)(2,1)}, bf16[1,64,2048]{2,1,0:T(8,128)(2,1)S(1)}, u32[]{:S(2)}, u32[]{:S(2)}) %collective-permute-start.1) | collective-permute-done | bytes 262176 | tf_op jit(solution)/shard_map/ppermute | solution.py:240
  227.8 8.1 %collective-permute-done = bf16[1,64,2048]{2,1,0:T(8,128)(2,1)S(1)} collective-permute-done((bf16[1,64,2048]{2,1,0:T(8,128)(2,1)}, bf16[1,64,2048]{2,1,0:T(8,128)(2,1)S(1)}, u32[]{:S(2)}, u32[]{:S(2)}) %collective-permute-start) | collective-permute-done | bytes 262176 | tf_op jit(solution)/shard_map/ppermute | solution.py:240
  235.8 0.7 copy.19
  236.5 0.7 copy.20
Async XLA Ops:
  134.2 8.3 %copy-start = (f32[1,64,8]{1,2,0:T(8,128)S(1)}, f32[1,64,8]{1,2,0:T(8,128)}, u32[]{:S(2)}) copy-start(f32[1,64,8]{1,2,0:T(8,128)} %param.17) | copy-start | bytes 6148
  134.2 9.0 %copy-start.1 = (f32[1,64,8]{1,2,0:T(8,128)S(1)}, f32[1,64,8]{1,2,0:T(8,128)}, u32[]{:S(2)}) copy-start(f32[1,64,8]{1,2,0:T(8,128)} %param.13) | copy-start | bytes 6148
  134.2 72.3 %all-to-all-start.1 = ((bf16[64,8,5120]{2,1,0:T(8,128)(2,1)}), bf16[64,8,5120]{2,1,0:T(8,128)(2,1)}, u32[]{:S(2)}, u32[]{:S(2)}) async-start(bf16[64,8,5120]{2,1,0:T(8,128)(2,1)} %bitcast.18), calls=%async_computation.1 | async-start | bytes 10485760 | tf_op jit(solution)/shard_map/all_to_all | solution.py:301
  210.4 17.4 %collective-permute-start.1 = (bf16[1,64,2048]{2,1,0:T(8,128)(2,1)}, bf16[1,64,2048]{2,1,0:T(8,128)(2,1)S(1)}, u32[]{:S(2)}, u32[]{:S(2)}) collective-permute-start(bf16[1,64,2048]{2,1,0:T(8,128)(2,1)} %bitcast.32), channel_id=1, source_target_pairs={{0,192},{64,0},{128,64},{192,128},{1,193},{65,1},{129,65},{193,129... | collective-permute-start | bytes 786440 | tf_op jit(solution)/shard_map/ppermute | solution.py:240
  219.4 16.4 %collective-permute-start = (bf16[1,64,2048]{2,1,0:T(8,128)(2,1)}, bf16[1,64,2048]{2,1,0:T(8,128)(2,1)S(1)}, u32[]{:S(2)}, u32[]{:S(2)}) collective-permute-start(bf16[1,64,2048]{2,1,0:T(8,128)(2,1)} %bitcast.33), channel_id=1, source_target_pairs={{0,64},{64,128},{128,192},{192,0},{1,65},{65,129},{129,193},{193,1... | collective-permute-start | bytes 786440 | tf_op jit(solution)/shard_map/ppermute | solution.py:240

commit v2 on v1

v2 whole, which is shorter than its diff:
```python
import jax
import jax.numpy as jnp
from jax import lax
from jax.experimental import pallas as pl
from jax.experimental.pallas import tpu as pltpu
from jax.sharding import PartitionSpec as P

EPSILON = 1e-06
BF = jnp.bfloat16
F32 = jnp.float32
SLOTS = 5
ROWS = 4
NN = (((1,), (0,)), ((), ()))
NT = (((1,), (1,)), ((), ()))
TN = (((0,), (0,)), ((), ()))


def dot(left, right, dims=NN):
    return lax.dot_general(left, right, dims, preferred_element_type=F32)


def iota(shape, axis):
    return lax.broadcasted_iota(jnp.int32, shape, axis)


def onehot(mask):
    return jnp.where(mask, 1.0, 0.0).astype(BF)


def slot_marks(routes, experts):
    top, tokens = routes.shape
    ids = iota((experts, tokens), 0)
    member = jnp.zeros((experts, tokens), F32)
    for k in range(top):
        member = jnp.where(routes[k : k + 1] == ids, 1.0, member)
    upto = onehot(iota((tokens, tokens), 0) <= iota((tokens, tokens), 1))
    return (dot(member.astype(BF), upto) * member).astype(BF)


def spread_rows(experts):
    rows = experts * ROWS
    return onehot(iota((rows, experts), 0) // ROWS == iota((rows, experts), 1))


def normalize(inputs, norm_scale):
    values = inputs.astype(F32)
    inv_rms = lax.rsqrt(jnp.mean(values * values, axis=-1, keepdims=True) + EPSILON)
    return values * inv_rms * norm_scale, values, inv_rms


def sub(shape):
    return iota(shape, 0) % (2 * ROWS)


def pack_kernel(experts, fwd, bwd, cot, fwd_routes, bwd_routes, gain, out, tile, sems):
    tokens, width = fwd.shape
    quarter = width // ROWS
    rows = experts * ROWS
    copies = []

    def send(at, values):
        cols = pl.ds(at * quarter, quarter)
        tile[:, cols] = values.astype(BF)
        copy = pltpu.make_async_copy(tile.at[:, cols], out.at[:, cols], sems.at[at])
        copy.start()
        copies.append(copy)

    fwd_marks = slot_marks(fwd_routes[...], experts)
    bwd_marks = slot_marks(bwd_routes[...], experts)
    i = iota((rows, experts), 0) // (2 * ROWS)
    e = iota((rows, experts), 1)
    marks = jnp.concatenate([fwd_marks, bwd_marks], axis=1)
    table = [dot(onehot(e == 2 * i + odd), marks) for odd in range(2)]
    pair = (rows, 2 * tokens)
    slot = (sub(pair) % ROWS + 1).astype(F32)
    low = sub(pair) < ROWS
    is_fwd = iota(pair, 1) < tokens
    fwd_rows = normalize(fwd[...], gain[...])[0].astype(BF)
    bwd_rows = normalize(bwd[...], gain[...])[0].astype(BF)
    cot_rows = cot[...]
    both = jnp.concatenate([fwd_rows, bwd_rows], axis=0)
    picks = [
        onehot((table[0] == slot) & (low == is_fwd)),
        onehot((table[1] == slot) & (low != is_fwd)),
    ]
    for block in range(2):
        for q in range(ROWS):
            part = slice(q * quarter, (q + 1) * quarter)
            send(block * ROWS + q, dot(picks[block], both[:, part]))
    crossed = jnp.where(low, table[1], table[0])
    crossed = onehot((crossed == slot) & jnp.logical_not(is_fwd))
    cots = jnp.concatenate([jnp.zeros_like(cot_rows), cot_rows], axis=0)
    for q in range(ROWS):
        part = slice(q * quarter, (q + 1) * quarter)
        send(2 * ROWS + q, dot(crossed, cots[:, part]))
    stacked = [
        jnp.concatenate([v[:, q * quarter : (q + 1) * quarter] for q in range(ROWS)], axis=0)
        for v in (fwd_rows, bwd_rows, cot_rows)
    ]
    spread = spread_rows(experts)
    four = (rows, ROWS * tokens)
    mine = iota(four, 0) % ROWS == iota(four, 1) // tokens
    for a, marks in enumerate((fwd_marks, bwd_marks, bwd_marks)):
        if a < 2:
            wide_table = dot(spread, jnp.concatenate([marks] * ROWS, axis=1))
            last = onehot((wide_table == SLOTS) & mine)
        send(3 * ROWS + a, dot(last, stacked[a]))
    for copy in copies:
        copy.wait()


def prepare_kernel(experts, *refs):
    for routes, weights, out in zip(refs[0:2], refs[2:4], refs[4:6]):
        top, tokens = routes.shape
        rows = experts * ROWS
        routes = routes[...]
        weights = weights[...]
        table = dot(spread_rows(experts), slot_marks(routes, experts))
        row = iota((rows, tokens), 0)
        owner = row // ROWS
        place = row % ROWS
        factor = jnp.zeros((rows, tokens), F32)
        for k in range(top):
            factor = jnp.where(routes[k : k + 1] == owner, weights[k : k + 1], factor)
        high = factor.astype(BF).astype(F32)
        eye = onehot(iota((rows, rows), 0) == iota((rows, rows), 1))
        at = 0
        for half in (high, factor - high):
            picked = jnp.where(table == (place + 1).astype(F32), half, 0.0).astype(BF)
            out[pl.ds(at, tokens), :] = dot(picked, eye, TN).astype(BF)
            at += tokens
        for q in range(ROWS):
            for half in (high, factor - high):
                picked = jnp.where((table == SLOTS) & (place == q), half, 0.0).astype(BF)
                out[pl.ds(at, tokens), :] = dot(picked, eye, TN).astype(BF)
                at += tokens


def tiles_of(values):
    grouped = values.reshape(values.shape[0] // 16, 2, 8, values.shape[1])
    return grouped[:, 0], grouped[:, 1]


def turn(values):
    return pltpu.roll(values, ROWS, 1)


def is_low(values):
    return iota(values.shape, 1) < ROWS


def half_rows(values, upper):
    even, odd = tiles_of(values)
    if upper:
        joined = jnp.where(is_low(even), turn(even), odd)
    else:
        joined = jnp.where(is_low(even), even, turn(odd))
    return joined.reshape(values.shape[0] // 2, values.shape[1])


def weave(lower, upper):
    shape = (lower.shape[0] // 8, 8, lower.shape[1])
    lower = lower.reshape(shape)
    upper = upper.reshape(shape)
    even = jnp.where(is_low(lower), lower, turn(upper))
    odd = jnp.where(is_low(lower), turn(lower), upper)
    return jnp.stack([even, odd], axis=1).reshape(2 * shape[0] * 8, shape[2])


def expert_kernel(
    arrived, w_gate, w_up, w_down, out, x, ends, gate_up, down, gu, h, act, grad, lasts, tile,
    in_sems, out_sems,
):
    local, width, hidden = w_gate.shape
    quarter = width // ROWS
    total = arrived.shape[0]
    groups = total // (local * ROWS)
    bulk = groups * ROWS
    loads = [pltpu.make_async_copy(arrived.at[:, pl.ds(3 * width, 3 * quarter)], ends, in_sems.at[0])]
    for block in range(3):
        loads.append(
            pltpu.make_async_copy(
                arrived.at[:, pl.ds(block * width, width)],
                x.at[block, pl.ds(0, total), :],
                in_sems.at[1 + block],
            )
        )
    weights = []
    for e in range(local):
        weights.append(
            pltpu.make_async_copy(w_gate.at[e], gate_up.at[e, :, pl.ds(0, hidden)], in_sems.at[4 + 3 * e])
        )
        weights.append(
            pltpu.make_async_copy(w_up.at[e], gate_up.at[e, :, pl.ds(hidden, hidden)], in_sems.at[5 + 3 * e])
        )
        weights.append(
            pltpu.make_async_copy(w_down.at[e], down.at[pl.ds(e * hidden, hidden), :], in_sems.at[6 + 3 * e])
        )
    for load in (
        loads[0], loads[1], weights[0], weights[1], loads[2], weights[3], weights[4], loads[3],
        weights[2], weights[5],
    ):
        load.start()

    c = iota((total, total), 1)
    r = iota((total, total), 0)
    where_from = (r % groups) * (local * ROWS) + r // groups
    loads[0].wait()
    rest = dot(onehot(c == where_from), ends[...]).astype(BF)
    for a, e, block, place in (
        (0, 0, 0, 0), (1, 0, 0, 1), (1, 1, 1, 0), (0, 1, 1, 1), (2, 1, 2, 0), (2, 0, 2, 1),
    ):
        for q in range(ROWS):
            at = (e * ROWS + q) * groups
            x[block, pl.ds(total + place * groups, groups), pl.ds(q * quarter, quarter)] = rest[
                at : at + groups, a * quarter : (a + 1) * quarter
            ]

    step = 2 * hidden // 3
    for load in (loads[1], weights[0], weights[1], loads[2], weights[3], weights[4]):
        load.wait()

    def gate_up_part(n, carry):
        e, cols = n // 3, pl.ds(pl.multiple_of((n % 3) * step, step), step)
        gu[e, :, cols] = dot(x[e], gate_up[e, :, cols])
        return carry

    lax.fori_loop(0, 3 * local, gate_up_part, 0)
    for load in (loads[3], weights[2], weights[5]):
        load.wait()

    def hidden_part(n, carry):
        cols = pl.ds(pl.multiple_of(n * step, step), step)
        h[:, cols] = dot(x[2], down[cols, :], NT)
        return carry

    lax.fori_loop(0, 3, hidden_part, 0)

    for e in range(local):
        def take(ref_values, forward):
            upper = forward == (e == 1)
            main = half_rows(ref_values[:total], upper)
            at = total + groups * int(upper)
            return jnp.concatenate([main, ref_values[at : at + groups]], axis=0)

        for n in range(3):
            cols = slice(n * hidden // 3, (n + 1) * hidden // 3)
            at = n * hidden // 3
            g_all = gu[e, :, pl.ds(at, hidden // 3)]
            u_all = gu[e, :, pl.ds(hidden + at, hidden // 3)]
            g = take(g_all, True)
            u = take(u_all, True)
            act[e, :, cols] = (g * jax.nn.sigmoid(g) * u).astype(BF)
            g = take(g_all, False)
            u = take(u_all, False)
            b = take(h[:, pl.ds(e * hidden + at, hidden // 3)], False)
            s = jax.nn.sigmoid(g)
            grad[e, :, cols] = (b * u * s * (1.0 + g * (1.0 - s))).astype(BF)
            grad[e, :, pl.ds(hidden + at, hidden // 3)] = (b * g * s).astype(BF)

    copies = []

    def ship(at, count):
        cols = pl.ds(at * quarter, count * quarter)
        copy = pltpu.make_async_copy(tile.at[:, cols], out.at[:, cols], out_sems.at[at])
        copy.start()
        copies.append(copy)

    for a in range(2):
        for q in range(ROWS):
            part = pl.ds(q * quarter, quarter)
            if a == 0:
                o = [dot(act[e], down[pl.ds(e * hidden, hidden), part]) for e in range(local)]
            else:
                o = [dot(grad[e], gate_up[e, part, :], NT) for e in range(local)]
            tile[:, pl.ds((a * ROWS + q) * quarter, quarter)] = weave(o[0][:bulk], o[1][:bulk]).astype(BF)
            for e in range(local):
                lasts[pl.ds((e * ROWS + q) * groups, groups), pl.ds(a * quarter, quarter)] = o[e][
                    bulk:
                ].astype(BF)
            ship(a * ROWS + q, 1)
    where_to = (c % groups) * (local * ROWS) + c // groups
    tile[:, pl.ds(2 * width, 2 * quarter)] = dot(onehot(r == where_to), lasts[...]).astype(BF)
    ship(2 * ROWS, 2)
    for copy in copies:
        copy.wait()


def weighted_sum(part, loads, matrix, tile):
    tokens = matrix.shape[0] // (2 + 2 * ROWS)
    quarter = tile.shape[1] // (2 * ROWS + 2)
    pieces = []
    for q in range(ROWS):
        at = part * ROWS + q
        loads[at].wait()
        piece = dot(matrix[pl.ds(0, 2 * tokens), :], tile[:, pl.ds(at * quarter, quarter)])
        pieces.append(piece[:tokens] + piece[tokens:])
    at = 2 * ROWS + part
    loads[at].wait()
    extra = dot(
        matrix[pl.ds(2 * tokens, 2 * ROWS * tokens), :], tile[:, pl.ds(at * quarter, quarter)]
    )
    for q in range(ROWS):
        at = 2 * q * tokens
        pieces[q] += extra[at : at + tokens] + extra[at + tokens : at + 2 * tokens]
    return jnp.concatenate(pieces, axis=1)


def combine_kernel(*refs):
    (returned, hbm_others, outs, tile, others, sems) = (
        refs[0], refs[1:7], refs[7:9], refs[9], refs[10:16], refs[16],
    )
    quarter = tile.shape[1] // (2 * ROWS + 2)
    chunks = 2 * ROWS + 2
    loads = [
        pltpu.make_async_copy(
            returned.at[:, pl.ds(at * quarter, quarter)],
            tile.at[:, pl.ds(at * quarter, quarter)],
            sems.at[at],
        )
        for at in range(chunks)
    ]
    more = [
        pltpu.make_async_copy(source, target, sems.at[chunks + i])
        for i, (source, target) in enumerate(zip(hbm_others, others))
    ]
    bwd_matrix, fwd_matrix, bwd_inputs, cot, fwd_inputs, gain = others
    half = list(range(ROWS, 2 * ROWS)) + [2 * ROWS + 1]
    rest = list(range(ROWS)) + [2 * ROWS]
    order = [more[0]] + [loads[at] for at in half] + more[2:4] + [more[5], more[1]]
    for load in order + [loads[at] for at in rest] + [more[4]]:
        load.start()
    more[0].wait()
    norm_grad = weighted_sum(1, loads, bwd_matrix, tile)
    for i in (2, 3, 5):
        more[i].wait()
    norm_scale = gain[...]
    _, values, inv_rms = normalize(bwd_inputs[...], norm_scale)
    scaled = norm_scale * norm_grad
    mean = jnp.mean(values * scaled, axis=-1, keepdims=True)
    outs[1][...] = (
        cot[...].astype(F32) + inv_rms * scaled - values * (inv_rms * inv_rms * inv_rms) * mean
    ).astype(BF)
    more[1].wait()
    combined = weighted_sum(0, loads, fwd_matrix, tile)
    more[4].wait()
    outs[0][...] = (fwd_inputs[...].astype(F32) + combined).astype(BF)


def from_behind(value, axis, steps):
    count = lax.axis_size(axis)
    pairs = [(source, (source + steps) % count) for source in range(count)]
    return lax.ppermute(value, axis, pairs)


def body(
    fwd_inputs,
    fwd_routes,
    fwd_weights,
    bwd_inputs,
    bwd_cotangent,
    bwd_routes,
    bwd_weights,
    norm_gain,
    w_gate,
    w_up,
    w_down,
):
    _, tokens, width = fwd_inputs.shape
    local = w_gate.shape[1]
    hidden = w_gate.shape[3]
    group = lax.axis_size("dp") * lax.axis_size("expert")
    experts = local * group
    rows = experts * ROWS
    quarter = width // ROWS
    wide = width + quarter
    bulk = group * ROWS
    vmem = pl.BlockSpec(memory_space=pltpu.VMEM)
    hbm = pl.BlockSpec(memory_space=pl.ANY)
    limit = pltpu.CompilerParams(vmem_limit_bytes=65_000_000)
    fwd_routes = fwd_routes[0].T
    bwd_routes = bwd_routes[0].T
    fwd_weights = fwd_weights[0].T
    bwd_weights = bwd_weights[0].T

    def cost(flops, moved):
        return pl.CostEstimate(flops=int(flops), bytes_accessed=int(moved), transcendentals=0)

    def exchange(packed):
        return lax.all_to_all(packed, ("dp", "expert"), split_axis=0, concat_axis=0, tiled=True)

    packed = pl.pallas_call(
        lambda *refs: pack_kernel(experts, *refs),
        out_shape=jax.ShapeDtypeStruct((rows, 3 * wide), BF),
        in_specs=[vmem] * 6,
        out_specs=hbm,
        scratch_shapes=[
            pltpu.VMEM((rows, 3 * wide), BF),
            pltpu.SemaphoreType.DMA((3 * (ROWS + 1),)),
        ],
        compiler_params=limit,
        cost_estimate=cost(9e9, 9e6),
        name="pack",
    )(fwd_inputs[0], bwd_inputs[0], bwd_cotangent[0], fwd_routes, bwd_routes, norm_gain)
    arrived = exchange(packed)
    matrix_shape = jax.ShapeDtypeStruct(((2 + 2 * ROWS) * tokens, rows), BF)
    fwd_matrix, bwd_matrix = pl.pallas_call(
        lambda *refs: prepare_kernel(experts, *refs),
        out_shape=(matrix_shape, matrix_shape),
        in_specs=[vmem] * 4,
        out_specs=(vmem, vmem),
        compiler_params=limit,
        cost_estimate=cost(4e9, 2e6),
        name="prepare",
    )(fwd_routes, bwd_routes, fwd_weights, bwd_weights)
    total = rows + 2 * group
    worked = pl.pallas_call(
        expert_kernel,
        out_shape=jax.ShapeDtypeStruct((rows, 2 * wide), BF),
        in_specs=[hbm] * 4,
        out_specs=hbm,
        scratch_shapes=[
            pltpu.VMEM((3, total, width), BF),
            pltpu.VMEM((rows, 3 * quarter), BF),
            pltpu.VMEM((local, width, 2 * hidden), BF),
            pltpu.VMEM((local * hidden, width), BF),
            pltpu.VMEM((local, total, 2 * hidden), F32),
            pltpu.VMEM((total, local * hidden), F32),
            pltpu.VMEM((local, bulk + group, hidden), BF),
            pltpu.VMEM((local, bulk + group, 2 * hidden), BF),
            pltpu.VMEM((rows, 2 * quarter), BF),
            pltpu.VMEM((rows, 2 * wide), BF),
            pltpu.SemaphoreType.DMA((4 + 3 * local,)),
            pltpu.SemaphoreType.DMA((2 * ROWS + 1,)),
        ],
        compiler_params=limit,
        cost_estimate=cost(20e9, 22e6),
        name="experts",
    )(arrived, w_gate[0], w_up[0], w_down[0])
    returned = exchange(worked)

    one = jax.ShapeDtypeStruct((tokens, width), BF)
    others = (bwd_matrix, fwd_matrix, bwd_inputs[0], bwd_cotangent[0], fwd_inputs[0], norm_gain)
    section_out, section_grad = pl.pallas_call(
        combine_kernel,
        out_shape=(one, one),
        in_specs=[hbm] * 7,
        out_specs=(vmem, vmem),
        scratch_shapes=[pltpu.VMEM((rows, 2 * wide), BF)]
        + [pltpu.VMEM(other.shape, other.dtype) for other in others]
        + [pltpu.SemaphoreType.DMA((2 * ROWS + 2 + len(others),))],
        compiler_params=limit,
        cost_estimate=cost(4e9, 8e6),
        name="combine",
    )(returned, *others)
    next_forward = from_behind(section_out[None], "segment", 1)
    prev_grad = from_behind(section_grad[None], "segment", -1)
    return (next_forward, prev_grad)


def solution(mesh):
    token = P("segment", ("dp", "expert"), None)
    weight = P("segment", ("dp", "expert"), None, None)
    return jax.shard_map(
        body,
        mesh=mesh,
        in_specs=(token,) * 7 + (P("segment", None),) + (weight,) * 3,
        out_specs=(token, token),
        check_vma=False,
    )
```

time: 238 us -> 223 us (0.937); the launches traced: 237 us -> 219 us
  Pallas kernels: 39.1 us -> 31.9 us
  waiting for transfers between devices: 79.1 us -> 72.1 us
  local copies, waits for them, and re-layouts: 5.54 us -> 1.41 us
    pallas_call x1, Pallas kernels: 25.9 us -> 18.2 us  [body(): pl.pallas_call(expert_kernel, out_shape=jax.ShapeDtypeStruct((rows, 2 * w...]
    unnamed x10 -> x2, local copies, waits for them, and re-layouts: 5.54 us -> 1.41 us
    ppermute x2, waiting for transfers between devices: 16.4 us -> 12.3 us  [from_behind(): return lax.ppermute(value, axis, pairs)]
    all_to_all x1, waiting for transfers between devices: 62.6 us -> 59.8 us  [exchange(): lax.all_to_all(packed, ('dp', 'expert'), split_axis=0, concat_axis=0, til...]
  transfers between devices with their start and end apart: 3 -> 3, of which waited for: 3 -> 2; matrix products, arithmetic and copies ran while one was open for 1% -> 0% of each run, Pallas kernels for 2% -> 2%
where the time goes in v2:
time: 223 us; the launch traced here: 219 us
  blocking collectives  99.1 us (44%)
  waiting for transfers between devices  72.1 us (32%)
  Pallas kernels  31.9 us (14%)
  starting transfers between devices  13.8 us (6%)
    all_to_all x1, blocking collectives, exchange(): lax.all_to_all(packed, ('dp', 'expert'), split_axis=0, concat_axis=0, til...  99.1 us
    all_to_all x1, waiting for transfers between devices, exchange(): lax.all_to_all(packed, ('dp', 'expert'), split_axis=0, concat_axis=0, til...  59.8 us
    pallas_call x1, Pallas kernels, body(): pl.pallas_call(expert_kernel, out_shape=jax.ShapeDtypeStruct((rows, 2 * w...  18.2 us
    ppermute x2, waiting for transfers between devices, from_behind(): return lax.ppermute(value, axis, pairs)  12.3 us
    all_to_all x1, starting transfers between devices, exchange(): lax.all_to_all(packed, ('dp', 'expert'), split_axis=0, concat_axis=0, til...  8.28 us
    ppermute x2, starting transfers between devices, from_behind(): return lax.ppermute(value, axis, pairs)  5.57 us
    pallas_call x1, Pallas kernels, body(): pl.pallas_call(lambda *refs: pack_kernel(experts, *refs), out_shape=jax.S...  5.08 us
  transfers between devices with their start and end apart: 3, of which 2 were waited for; matrix products, arithmetic and copies ran while one was open for 0% of the time, Pallas kernels for 2%

profile of v2, /device:TPU:32, one launch (start us, length us, event | category | flops | bytes accessed | tf_op | source)
XLA Modules:
  0.0 219.1 jit_solution(3399701677779242467)
XLA Ops:
  0.6 5.1 %pack.1 = bf16[512,7680]{1,0:T(8,128)(2,1)} custom-call(bf16[64,2048]{1,0:T(8,128)(2,1)} %bitcast.30, bf16[64,2048]{1,0:T(8,128)(2,1)} %bitcast.32, bf16[64,2048]{1,0:T(8,128)(2,1)} %bitcast.34, s32[8,64]{1,0:T(8,128)} %bitcast.38, s32[8,64]{1,0:T(8,128)} %bitcast.40, f32[1,2048]{1,0:T(1,128)} %refs_6_.1), custom_call_target="tpu_custom_call" | custom-call | flops 8999999488 | bytes 9000000 | tf_op jit(solution)/shard_map/pack/pallas_call | solution.py:392
  5.7 99.1 %all_to_all.22 = bf16[64,8,7680]{2,1,0:T(8,128)(2,1)} all-to-all(bf16[64,8,7680]{2,1,0:T(8,128)(2,1)} %bitcast.25), channel_id=1, replica_groups=mesh['segment'=4,'dp'=4,'expert'=16] {'dp','expert'}, dimensions={0} | all-to-all | bytes 15728640 | tf_op jit(solution)/shard_map/all_to_all | solution.py:390
  104.9 18.2 %experts.1 = bf16[512,5120]{1,0:T(8,128)(2,1)} custom-call(bf16[512,7680]{1,0:T(8,128)(2,1)} %bitcast.24, bf16[2,2048,384]{2,1,0:T(8,128)(2,1)} %bitcast.27, bf16[2,2048,384]{2,1,0:T(8,128)(2,1)} %bitcast.28, bf16[2,384,2048]{2,1,0:T(8,128)(2,1)} %bitcast.29), custom_call_target="tpu_custom_call" | custom-call | flops 20000000000 | bytes 22000000 | tf_op jit(solution)/shard_map/experts/pallas_call | solution.py:417
  123.0 8.3 %all-to-all-start.1 = ((bf16[64,8,5120]{2,1,0:T(8,128)(2,1)}), bf16[64,8,5120]{2,1,0:T(8,128)(2,1)}, u32[]{:S(2)}, u32[]{:S(2)}) async-start(bf16[64,8,5120]{2,1,0:T(8,128)(2,1)} %bitcast.26), calls=%async_computation.1 | async-start | bytes 10485760 | tf_op jit(solution)/shard_map/all_to_all | solution.py:390
  131.3 4.2 %prepare.1 = (bf16[640,512]{1,0:T(8,128)(2,1)}, bf16[640,512]{1,0:T(8,128)(2,1)}) custom-call(s32[8,64]{1,0:T(8,128)} %bitcast.39, s32[8,64]{1,0:T(8,128)} %bitcast.41, f32[8,64]{1,0:T(8,128)} %bitcast.42, f32[8,64]{1,0:T(8,128)} %bitcast.43), custom_call_target="tpu_custom_call" | custom-call | flops 4000000000 | bytes 2000000 | tf_op jit(solution)/shard_map/prepare/pallas_call | solution.py:407
  135.5 59.8 %all-to-all-done.1 = bf16[64,8,5120]{2,1,0:T(8,128)(2,1)} async-done(((bf16[64,8,5120]{2,1,0:T(8,128)(2,1)}), bf16[64,8,5120]{2,1,0:T(8,128)(2,1)}, u32[]{:S(2)}, u32[]{:S(2)}) %all-to-all-start.1) | async-done | bytes 5242912 | tf_op jit(solution)/shard_map/all_to_all | solution.py:390
  195.3 4.4 %combine.1 = (bf16[64,2048]{1,0:T(8,128)(2,1)}, bf16[64,2048]{1,0:T(8,128)(2,1)}) custom-call(bf16[512,5120]{1,0:T(8,128)(2,1)} %bitcast.13.refs_0_, bf16[640,512]{1,0:T(8,128)(2,1)} %get-tuple-element.6.refs_1_, bf16[640,512]{1,0:T(8,128)(2,1)} %get-tuple-element.7.refs_2_, bf16[64,2048]{1,0:T(8,128)(2,1)} %bitcast.33, bf16[64,2048]{1,0:T(8,128)(2,1)} %bitcast.35, ...), custom_call_target="tpu_custom_call" | custom-call | flops 4000000000 | bytes 8000000 | tf_op jit(solution)/shard_map/combine/pallas_call | solution.py:444
  199.8 3.3 %collective-permute-start = (bf16[1,64,2048]{2,1,0:T(8,128)(2,1)}, bf16[1,64,2048]{2,1,0:T(8,128)(2,1)S(1)}, u32[]{:S(2)}, u32[]{:S(2)}) collective-permute-start(bf16[1,64,2048]{2,1,0:T(8,128)(2,1)} %bitcast.37), channel_id=1, source_target_pairs={{0,64},{64,128},{128,192},{192,0},{1,65},{65,129},{129,193},{193,1... | collective-permute-start | bytes 786440 | tf_op jit(solution)/shard_map/ppermute | solution.py:353
  203.1 2.2 %collective-permute-start.1 = (bf16[1,64,2048]{2,1,0:T(8,128)(2,1)}, bf16[1,64,2048]{2,1,0:T(8,128)(2,1)S(1)}, u32[]{:S(2)}, u32[]{:S(2)}) collective-permute-start(bf16[1,64,2048]{2,1,0:T(8,128)(2,1)} %bitcast.36), channel_id=1, source_target_pairs={{0,192},{64,0},{128,64},{192,128},{1,193},{65,1},{129,65},{193,129... | collective-permute-start | bytes 786440 | tf_op jit(solution)/shard_map/ppermute | solution.py:353
  205.4 12.3 %collective-permute-done = bf16[1,64,2048]{2,1,0:T(8,128)(2,1)S(1)} collective-permute-done((bf16[1,64,2048]{2,1,0:T(8,128)(2,1)}, bf16[1,64,2048]{2,1,0:T(8,128)(2,1)S(1)}, u32[]{:S(2)}, u32[]{:S(2)}) %collective-permute-start) | collective-permute-done | bytes 262176 | tf_op jit(solution)/shard_map/ppermute | solution.py:353
  217.6 0.0 collective-permute-done.1
  217.7 0.7 copy.15
  218.4 0.7 copy.16
Async XLA Ops:
  123.0 72.3 %all-to-all-start.1 = ((bf16[64,8,5120]{2,1,0:T(8,128)(2,1)}), bf16[64,8,5120]{2,1,0:T(8,128)(2,1)}, u32[]{:S(2)}, u32[]{:S(2)}) async-start(bf16[64,8,5120]{2,1,0:T(8,128)(2,1)} %bitcast.26), calls=%async_computation.1 | async-start | bytes 10485760 | tf_op jit(solution)/shard_map/all_to_all | solution.py:390
  199.8 17.9 %collective-permute-start = (bf16[1,64,2048]{2,1,0:T(8,128)(2,1)}, bf16[1,64,2048]{2,1,0:T(8,128)(2,1)S(1)}, u32[]{:S(2)}, u32[]{:S(2)}) collective-permute-start(bf16[1,64,2048]{2,1,0:T(8,128)(2,1)} %bitcast.37), channel_id=1, source_target_pairs={{0,64},{64,128},{128,192},{192,0},{1,65},{65,129},{129,193},{193,1... | collective-permute-start | bytes 786440 | tf_op jit(solution)/shard_map/ppermute | solution.py:353
  203.1 14.5 %collective-permute-start.1 = (bf16[1,64,2048]{2,1,0:T(8,128)(2,1)}, bf16[1,64,2048]{2,1,0:T(8,128)(2,1)S(1)}, u32[]{:S(2)}, u32[]{:S(2)}) collective-permute-start(bf16[1,64,2048]{2,1,0:T(8,128)(2,1)} %bitcast.36), channel_id=1, source_target_pairs={{0,192},{64,0},{128,64},{192,128},{1,193},{65,1},{129,65},{193,129... | collective-permute-start | bytes 786440 | tf_op jit(solution)/shard_map/ppermute | solution.py:353

commit v3 on v2

v3 whole, which is shorter than its diff:
```python
import jax
import jax.numpy as jnp
from jax import lax
from jax.experimental import pallas as pl
from jax.experimental.pallas import tpu as pltpu
from jax.sharding import PartitionSpec as P


EPSILON = 1e-06
BF = jnp.bfloat16
F32 = jnp.float32
SLOTS = 5
ROWS = 4
NN = (((1,), (0,)), ((), ()))
NT = (((1,), (1,)), ((), ()))
TN = (((0,), (0,)), ((), ()))


def dot(left, right, dims=NN):
    return lax.dot_general(left, right, dims, preferred_element_type=F32)


def iota(shape, axis):
    return lax.broadcasted_iota(jnp.int32, shape, axis)


def onehot(mask):
    return jnp.where(mask, 1.0, 0.0).astype(BF)


def slot_marks(routes, experts):
    top, tokens = routes.shape
    ids = iota((experts, tokens), 0)
    member = jnp.zeros((experts, tokens), F32)
    for k in range(top):
        member = jnp.where(routes[k : k + 1] == ids, 1.0, member)
    upto = onehot(iota((tokens, tokens), 0) <= iota((tokens, tokens), 1))
    return (dot(member.astype(BF), upto) * member).astype(BF)


def spread_rows(experts):
    rows = experts * ROWS
    return onehot(iota((rows, experts), 0) // ROWS == iota((rows, experts), 1))


def normalize(inputs, norm_scale):
    values = inputs.astype(F32)
    inv_rms = lax.rsqrt(jnp.mean(values * values, axis=-1, keepdims=True) + EPSILON)
    return values * inv_rms * norm_scale, values, inv_rms


def sub(shape):
    return iota(shape, 0) % (2 * ROWS)


def pack_kernel(experts, fwd, bwd, cot, fwd_routes, bwd_routes, gain, out, tile, sems):
    tokens, width = fwd.shape
    quarter = width // ROWS
    rows = experts * ROWS
    copies = []

    def send(at, values):
        cols = pl.ds(at * quarter, quarter)
        tile[:, cols] = values.astype(BF)
        copy = pltpu.make_async_copy(tile.at[:, cols], out.at[:, cols], sems.at[at])
        copy.start()
        copies.append(copy)

    fwd_marks = slot_marks(fwd_routes[...], experts)
    bwd_marks = slot_marks(bwd_routes[...], experts)
    i = iota((rows, experts), 0) // (2 * ROWS)
    e = iota((rows, experts), 1)
    marks = jnp.concatenate([fwd_marks, bwd_marks], axis=1)
    table = [dot(onehot(e == 2 * i + odd), marks) for odd in range(2)]
    pair = (rows, 2 * tokens)
    slot = (sub(pair) % ROWS + 1).astype(F32)
    low = sub(pair) < ROWS
    is_fwd = iota(pair, 1) < tokens
    fwd_rows = normalize(fwd[...], gain[...])[0].astype(BF)
    bwd_rows = normalize(bwd[...], gain[...])[0].astype(BF)
    cot_rows = cot[...]
    both = jnp.concatenate([fwd_rows, bwd_rows], axis=0)
    picks = [
        onehot((table[0] == slot) & (low == is_fwd)),
        onehot((table[1] == slot) & (low != is_fwd)),
    ]
    for block in range(2):
        for q in range(ROWS):
            part = slice(q * quarter, (q + 1) * quarter)
            send(block * ROWS + q, dot(picks[block], both[:, part]))
    crossed = jnp.where(low, table[1], table[0])
    crossed = onehot((crossed == slot) & jnp.logical_not(is_fwd))
    cots = jnp.concatenate([jnp.zeros_like(cot_rows), cot_rows], axis=0)
    for q in range(ROWS):
        part = slice(q * quarter, (q + 1) * quarter)
        send(2 * ROWS + q, dot(crossed, cots[:, part]))
    stacked = [
        jnp.concatenate([v[:, q * quarter : (q + 1) * quarter] for q in range(ROWS)], axis=0)
        for v in (fwd_rows, bwd_rows, cot_rows)
    ]
    spread = spread_rows(experts)
    four = (rows, ROWS * tokens)
    mine = iota(four, 0) % ROWS == iota(four, 1) // tokens
    for a, marks in enumerate((fwd_marks, bwd_marks, bwd_marks)):
        if a < 2:
            wide_table = dot(spread, jnp.concatenate([marks] * ROWS, axis=1))
            last = onehot((wide_table == SLOTS) & mine)
        send(3 * ROWS + a, dot(last, stacked[a]))
    for copy in copies:
        copy.wait()


def weight_matrix(routes, weights, experts):
    top, tokens = routes.shape
    rows = experts * ROWS
    ids = iota((experts, tokens), 0)
    factor = jnp.zeros((experts, tokens), F32)
    for k in range(top):
        factor = jnp.where(routes[k : k + 1] == ids, weights[k : k + 1], factor)
    high = factor.astype(BF)
    low = (factor - high.astype(F32)).astype(BF)
    spread = onehot(iota((experts, rows), 1) // ROWS == iota((experts, rows), 0))
    table = dot(jnp.concatenate([slot_marks(routes, experts), high, low], axis=1), spread, TN)
    slots, halves = table[:tokens], (table[tokens : 2 * tokens], table[2 * tokens :])
    place = iota((tokens, rows), 1) % ROWS
    parts = [jnp.where(slots == (place + 1).astype(F32), half, 0.0) for half in halves]
    for q in range(ROWS):
        parts.extend(jnp.where((slots == SLOTS) & (place == q), half, 0.0) for half in halves)
    return jnp.concatenate([part.astype(BF) for part in parts], axis=0)


def tiles_of(values):
    grouped = values.reshape(values.shape[0] // 16, 2, 8, values.shape[1])
    return grouped[:, 0], grouped[:, 1]


def turn(values):
    return pltpu.roll(values, ROWS, 1)


def is_low(values):
    return iota(values.shape, 1) < ROWS


def half_rows(values, upper):
    even, odd = tiles_of(values)
    if upper:
        joined = jnp.where(is_low(even), turn(even), odd)
    else:
        joined = jnp.where(is_low(even), even, turn(odd))
    return joined.reshape(values.shape[0] // 2, values.shape[1])


def weave(lower, upper):
    shape = (lower.shape[0] // 8, 8, lower.shape[1])
    lower = lower.reshape(shape)
    upper = upper.reshape(shape)
    even = jnp.where(is_low(lower), lower, turn(upper))
    odd = jnp.where(is_low(lower), turn(lower), upper)
    return jnp.stack([even, odd], axis=1).reshape(2 * shape[0] * 8, shape[2])


def expert_kernel(
    arrived, w_gate, w_up, down, out, x, ends, gate_up, gu, h, act, grad, lasts, tile, in_sems,
    out_sems,
):
    local, width, hidden = w_gate.shape
    quarter = width // ROWS
    total = arrived.shape[0]
    groups = total // (local * ROWS)
    bulk = groups * ROWS
    loads = [pltpu.make_async_copy(arrived.at[:, pl.ds(3 * width, 3 * quarter)], ends, in_sems.at[0])]
    for block in range(3):
        loads.append(
            pltpu.make_async_copy(
                arrived.at[:, pl.ds(block * width, width)],
                x.at[block, pl.ds(0, total), :],
                in_sems.at[1 + block],
            )
        )
    for load in loads:
        load.start()
    for i, source in enumerate((w_gate, w_up)):
        loads.append(
            pltpu.make_async_copy(
                source, gate_up.at[:, :, pl.ds(i * hidden, hidden)], in_sems.at[4 + i]
            )
        )
        loads[-1].start()
    c = iota((total, total), 1)
    r = iota((total, total), 0)
    where_from = (r % groups) * (local * ROWS) + r // groups
    loads[0].wait()
    rest = dot(onehot(c == where_from), ends[...]).astype(BF)
    for a, e, block, place in (
        (0, 0, 0, 0), (1, 0, 0, 1), (1, 1, 1, 0), (0, 1, 1, 1), (2, 1, 2, 0), (2, 0, 2, 1),
    ):
        for q in range(ROWS):
            at = (e * ROWS + q) * groups
            x[block, pl.ds(total + place * groups, groups), pl.ds(q * quarter, quarter)] = rest[
                at : at + groups, a * quarter : (a + 1) * quarter
            ]

    step = 2 * hidden // 3
    third = hidden // 3

    def gate_up_of(e):
        for n in range(3):
            cols = pl.ds(n * step, step)
            gu[e, :, cols] = dot(x[e], gate_up[e, :, cols])

    def take(values, e, forward):
        upper = forward == (e == 1)
        main = half_rows(values[:total], upper)
        at = total + groups * int(upper)
        return jnp.concatenate([main, values[at : at + groups]], axis=0)

    def forward_of(e):
        for at in range(0, hidden, third):
            g = take(gu[e, :, pl.ds(at, third)], e, True)
            u = take(gu[e, :, pl.ds(hidden + at, third)], e, True)
            act[e, :, pl.ds(at, third)] = (g * jax.nn.sigmoid(g) * u).astype(BF)

    def backward_of(e):
        for at in range(0, hidden, third):
            g = take(gu[e, :, pl.ds(at, third)], e, False)
            u = take(gu[e, :, pl.ds(hidden + at, third)], e, False)
            b = take(h[:, pl.ds(e * hidden + at, third)], e, False)
            s = jax.nn.sigmoid(g)
            grad[e, :, pl.ds(at, third)] = (b * u * s * (1.0 + g * (1.0 - s))).astype(BF)
            grad[e, :, pl.ds(hidden + at, third)] = (b * g * s).astype(BF)

    copies = []
    back_to = onehot(r == (c % groups) * (local * ROWS) + c // groups)

    def ship(at):
        cols = pl.ds(at * quarter, quarter)
        copy = pltpu.make_async_copy(tile.at[:, cols], out.at[:, cols], out_sems.at[at])
        copy.start()
        copies.append(copy)

    def send_back(a, q):
        part = pl.ds(q * quarter, quarter)
        if a == 0:
            o = [dot(act[e], down[pl.ds(e * hidden, hidden), part]) for e in range(local)]
        else:
            o = [dot(grad[e], gate_up[e, part, :], NT) for e in range(local)]
        tile[:, pl.ds((a * ROWS + q) * quarter, quarter)] = weave(o[0][:bulk], o[1][:bulk]).astype(BF)
        for e in range(local):
            lasts[pl.ds((e * ROWS + q) * groups, groups), pl.ds(a * quarter, quarter)] = o[e][
                bulk:
            ].astype(BF)
        ship(a * ROWS + q)

    def send_back_last(a):
        tile[:, pl.ds((2 * ROWS + a) * quarter, quarter)] = dot(
            back_to, lasts[:, pl.ds(a * quarter, quarter)]
        ).astype(BF)
        ship(2 * ROWS + a)

    for load in loads[1:3] + loads[4:]:
        load.wait()
    gate_up_of(0)
    gate_up_of(1)
    forward_of(0)
    loads[3].wait()
    for n in range(3):
        cols = pl.ds(n * step, step)
        h[:, cols] = dot(x[2], down[cols, :], NT)
    forward_of(1)
    for q in range(ROWS):
        send_back(0, q)
    backward_of(0)
    backward_of(1)
    send_back_last(0)
    for q in range(ROWS):
        send_back(1, q)
    send_back_last(1)
    for copy in copies:
        copy.wait()


def weighted_sum(part, returned, matrix):
    tokens = matrix.shape[0] // (2 + 2 * ROWS)
    quarter = returned.shape[1] // (2 * ROWS + 2)
    pieces = []
    for q in range(ROWS):
        at = part * ROWS + q
        piece = dot(matrix[: 2 * tokens], returned[:, pl.ds(at * quarter, quarter)])
        pieces.append(piece[:tokens] + piece[tokens:])
    at = 2 * ROWS + part
    extra = dot(matrix[2 * tokens :], returned[:, pl.ds(at * quarter, quarter)])
    for q in range(ROWS):
        at = 2 * q * tokens
        pieces[q] += extra[at : at + tokens] + extra[at + tokens : at + 2 * tokens]
    return jnp.concatenate(pieces, axis=1)


def combine_kernel(
    experts, returned, fwd_routes, bwd_routes, fwd_weights, bwd_weights, bwd_inputs, cot,
    fwd_inputs, gain, fwd_out, bwd_out,
):
    fwd_matrix = weight_matrix(fwd_routes[...], fwd_weights[...], experts)
    combined = weighted_sum(0, returned, fwd_matrix)
    fwd_out[...] = (fwd_inputs[...].astype(F32) + combined).astype(BF)
    bwd_matrix = weight_matrix(bwd_routes[...], bwd_weights[...], experts)
    norm_grad = weighted_sum(1, returned, bwd_matrix)
    norm_scale = gain[...]
    _, values, inv_rms = normalize(bwd_inputs[...], norm_scale)
    scaled = norm_scale * norm_grad
    mean = jnp.mean(values * scaled, axis=-1, keepdims=True)
    bwd_out[...] = (
        cot[...].astype(F32) + inv_rms * scaled - values * (inv_rms * inv_rms * inv_rms) * mean
    ).astype(BF)


def from_behind(value, axis, steps):
    count = lax.axis_size(axis)
    pairs = [(source, (source + steps) % count) for source in range(count)]
    return lax.ppermute(value, axis, pairs)


def body(
    fwd_inputs,
    fwd_routes,
    fwd_weights,
    bwd_inputs,
    bwd_cotangent,
    bwd_routes,
    bwd_weights,
    norm_gain,
    w_gate,
    w_up,
    w_down,
):
    _, tokens, width = fwd_inputs.shape
    local = w_gate.shape[1]
    hidden = w_gate.shape[3]
    group = lax.axis_size("dp") * lax.axis_size("expert")
    experts = local * group
    rows = experts * ROWS
    quarter = width // ROWS
    wide = width + quarter
    bulk = group * ROWS
    vmem = pl.BlockSpec(memory_space=pltpu.VMEM)
    hbm = pl.BlockSpec(memory_space=pltpu.HBM)
    limit = pltpu.CompilerParams(vmem_limit_bytes=65_000_000)
    fwd_routes = fwd_routes[0].T
    bwd_routes = bwd_routes[0].T
    fwd_weights = fwd_weights[0].T
    bwd_weights = bwd_weights[0].T

    def cost(flops, moved):
        return pl.CostEstimate(flops=int(flops), bytes_accessed=int(moved), transcendentals=0)

    def exchange(packed):
        return lax.all_to_all(packed, ("dp", "expert"), split_axis=0, concat_axis=0, tiled=True)

    packed = pl.pallas_call(
        lambda *refs: pack_kernel(experts, *refs),
        out_shape=jax.ShapeDtypeStruct((rows, 3 * wide), BF),
        in_specs=[vmem] * 6,
        out_specs=hbm,
        scratch_shapes=[
            pltpu.VMEM((rows, 3 * wide), BF),
            pltpu.SemaphoreType.DMA((3 * (ROWS + 1),)),
        ],
        compiler_params=limit,
        cost_estimate=cost(9e9, 9e6),
        name="pack",
    )(fwd_inputs[0], bwd_inputs[0], bwd_cotangent[0], fwd_routes, bwd_routes, norm_gain)
    arrived = exchange(packed)
    total = rows + 2 * group
    worked = pl.pallas_call(
        expert_kernel,
        out_shape=jax.ShapeDtypeStruct((rows, 2 * wide), BF),
        in_specs=[hbm] + [vmem] * 3,
        out_specs=hbm,
        scratch_shapes=[
            pltpu.VMEM((3, total, width), BF),
            pltpu.VMEM((rows, 3 * quarter), BF),
            pltpu.VMEM((local, width, 2 * hidden), BF),
            pltpu.VMEM((local, total, 2 * hidden), F32),
            pltpu.VMEM((total, local * hidden), F32),
            pltpu.VMEM((local, bulk + group, hidden), BF),
            pltpu.VMEM((local, bulk + group, 2 * hidden), BF),
            pltpu.VMEM((rows, 2 * quarter), BF),
            pltpu.VMEM((rows, 2 * wide), BF),
            pltpu.SemaphoreType.DMA((6,)),
            pltpu.SemaphoreType.DMA((2 * ROWS + 2,)),
        ],
        compiler_params=pltpu.CompilerParams(vmem_limit_bytes=40 * 1024 * 1024),
        cost_estimate=cost(20e9, 22e6),
        name="experts",
    )(
        arrived,
        w_gate[0],
        w_up[0],
        w_down[0].reshape(local * hidden, width),
    )
    returned = exchange(worked)

    one = jax.ShapeDtypeStruct((tokens, width), BF)
    section_out, section_grad = pl.pallas_call(
        lambda *refs: combine_kernel(experts, *refs),
        out_shape=(one, one),
        in_specs=[vmem] * 9,
        out_specs=(vmem, vmem),
        compiler_params=pltpu.CompilerParams(vmem_limit_bytes=16 * 1024 * 1024),
        cost_estimate=cost(4e9, 8e6),
        name="combine",
    )(
        returned,
        fwd_routes,
        bwd_routes,
        fwd_weights,
        bwd_weights,
        bwd_inputs[0],
        bwd_cotangent[0],
        fwd_inputs[0],
        norm_gain,
    )
    next_forward = from_behind(section_out[None], "segment", 1)
    prev_grad = from_behind(section_grad[None], "segment", -1)
    return (next_forward, prev_grad)


def solution(mesh):
    token = P("segment", ("dp", "expert"), None)
    weight = P("segment", ("dp", "expert"), None, None)
    return jax.shard_map(
        body,
        mesh=mesh,
        in_specs=(token,) * 7 + (P("segment", None),) + (weight,) * 3,
        out_specs=(token, token),
        check_vma=False,
    )
```

time: 223 us -> 216 us (0.969); the launches traced: 219 us -> 215 us
  blocking collectives: 99.1 us -> 170 us
  waiting for transfers between devices: 72.1 us -> 16 us
  Pallas kernels: 31.9 us -> 21.8 us
  starting transfers between devices: 13.8 us -> 5.47 us
    all_to_all x1 -> x2, blocking collectives: 99.1 us -> 170 us  [exchange(): lax.all_to_all(packed, ('dp', 'expert'), split_axis=0, concat_axis=0, til...]
    all_to_all x1 -> x0, waiting for transfers between devices: 59.8 us -> none  [exchange(): lax.all_to_all(packed, ('dp', 'expert'), split_axis=0, concat_axis=0, til...]
    all_to_all x1 -> x0, starting transfers between devices: 8.28 us -> none  [exchange(): lax.all_to_all(packed, ('dp', 'expert'), split_axis=0, concat_axis=0, til...]
    pallas_call x2 -> x1, Pallas kernels: 8.61 us -> 2.17 us  [body(): pl.pallas_call(lambda *refs: combine_kernel(experts, *refs), out_shape=(o...]
    ppermute x2, waiting for transfers between devices: 12.3 us -> 16 us  [from_behind(): return lax.ppermute(value, axis, pairs)]
    pallas_call x1, Pallas kernels: 18.2 us -> 14.5 us  [body(): pl.pallas_call(expert_kernel, out_shape=jax.ShapeDtypeStruct((rows, 2 * w...]
  transfers between devices with their start and end apart: 3 -> 2, of which waited for: 2 -> 2; matrix products, arithmetic and copies ran while one was open for 0% -> 0% of each run, Pallas kernels for 2% -> 0%
where the time goes in v3:
time: 216 us; the launch traced here: 215 us
  blocking collectives  170 us (79%)
  Pallas kernels  21.8 us (10%)
  waiting for transfers between devices  16 us (7%)
  starting transfers between devices  5.47 us (3%)
    all_to_all x2, blocking collectives, exchange(): lax.all_to_all(packed, ('dp', 'expert'), split_axis=0, concat_axis=0, til...  170 us
    ppermute x2, waiting for transfers between devices, from_behind(): return lax.ppermute(value, axis, pairs)  16 us
    pallas_call x1, Pallas kernels, body(): pl.pallas_call(expert_kernel, out_shape=jax.ShapeDtypeStruct((rows, 2 * w...  14.5 us
    ppermute x2, starting transfers between devices, from_behind(): return lax.ppermute(value, axis, pairs)  5.47 us
    pallas_call x1, Pallas kernels, body(): pl.pallas_call(lambda *refs: pack_kernel(experts, *refs), out_shape=jax.S...  5.09 us
  transfers between devices with their start and end apart: 2, of which 2 were waited for; matrix products, arithmetic and copies ran while one was open for 0% of the time, Pallas kernels for 0%

profile of v3, /device:TPU:32, one launch (start us, length us, event | category | flops | bytes accessed | tf_op | source)
XLA Modules:
  0.0 215.2 jit_solution(8073123449047499656)
XLA Ops:
  0.6 5.1 %pack.1 = bf16[512,7680]{1,0:T(8,128)(2,1)} custom-call(bf16[64,2048]{1,0:T(8,128)(2,1)} %bitcast.28, bf16[64,2048]{1,0:T(8,128)(2,1)} %bitcast.30, bf16[64,2048]{1,0:T(8,128)(2,1)} %bitcast.32, s32[8,64]{1,0:T(8,128)} %bitcast.36, s32[8,64]{1,0:T(8,128)} %bitcast.38, f32[1,2048]{1,0:T(1,128)} %refs_8_.1), custom_call_target="tpu_custom_call" | custom-call | flops 8999999488 | bytes 9000000 | tf_op jit(solution)/shard_map/pack/pallas_call | solution.py:359
  5.7 0.0 copy-start
  5.7 0.0 copy-start.1
  5.8 0.0 copy-start.2
  5.8 99.4 %all_to_all.22 = bf16[64,8,7680]{2,1,0:T(8,128)(2,1)} all-to-all(bf16[64,8,7680]{2,1,0:T(8,128)(2,1)} %bitcast.43), channel_id=1, replica_groups=mesh['segment'=4,'dp'=4,'expert'=16] {'dp','expert'}, dimensions={0} | all-to-all | bytes 15728640 | tf_op jit(solution)/shard_map/all_to_all | solution.py:357
  105.2 0.0 copy-done
  105.2 0.0 copy-done.1
  105.2 0.0 copy-done.2
  105.2 14.5 %experts.1 = bf16[512,5120]{1,0:T(8,128)(2,1)} custom-call(bf16[512,7680]{1,0:T(8,128)(2,1)} %bitcast.42, bf16[2,2048,384]{2,1,0:T(8,128)(2,1)S(1)} %bitcast.25, bf16[2,2048,384]{2,1,0:T(8,128)(2,1)S(1)} %bitcast.26, bf16[768,2048]{1,0:T(8,128)(2,1)S(1)} %bitcast.27), custom_call_target="tpu_custom_call" | custom-call | flops 20000000000 | bytes 22000000 | tf_op jit(solution)/shard_map/experts/pallas_call | solution.py:374
  119.7 0.0 copy-start.3
  119.7 0.0 copy-start.4
  119.7 0.0 copy-start.5
  119.7 0.0 copy-start.6
  119.8 0.0 copy-start.7
  119.8 0.0 copy-start.8
  119.8 0.0 copy-start.9
  119.8 0.0 copy-start.10
  119.8 70.3 %all_to_all.23 = bf16[64,8,5120]{2,1,0:T(8,128)(2,1)S(1)} all-to-all(bf16[64,8,5120]{2,1,0:T(8,128)(2,1)} %bitcast.44), channel_id=1, replica_groups=mesh['segment'=4,'dp'=4,'expert'=16] {'dp','expert'}, dimensions={0} | all-to-all | bytes 10485760 | tf_op jit(solution)/shard_map/all_to_all | solution.py:357
  190.1 0.0 copy-done.3
  190.1 0.0 copy-done.4
  190.1 0.0 copy-done.5
  190.1 0.0 copy-done.6
  190.1 0.0 copy-done.7
  190.1 0.0 copy-done.8
  190.1 0.0 copy-done.9
  190.2 2.2 %combine.1 = (bf16[64,2048]{1,0:T(8,128)(2,1)S(1)}, bf16[64,2048]{1,0:T(8,128)(2,1)S(1)}) custom-call(bf16[512,5120]{1,0:T(8,128)(2,1)S(1)} %bitcast.24, s32[8,64]{1,0:T(8,128)S(1)} %bitcast.37, s32[8,64]{1,0:T(8,128)S(1)} %bitcast.39, f32[8,64]{1,0:T(8,128)S(1)} %bitcast.40, f32[8,64]{1,0:T(8,128)S(1)} %bitcast.41, bf16[64,2048]{1,0:T(8,128)(2,1)S(1)} %bitcast.31, ...), custom_call_target="tpu_custom_call" | custom-call | flops 4000000000 | bytes 8000000 | tf_op jit(solution)/shard_map/combine/pallas_call | solution.py:404
  192.3 5.5 %collective-permute-start.1 = (bf16[1,64,2048]{2,1,0:T(8,128)(2,1)S(1)}, bf16[1,64,2048]{2,1,0:T(8,128)(2,1)S(1)}, u32[]{:S(2)}, u32[]{:S(2)}) collective-permute-start(bf16[1,64,2048]{2,1,0:T(8,128)(2,1)S(1)} %bitcast.35), channel_id=1, source_target_pairs={{0,192},{64,0},{128,64},{192,128},{1,193},{65,1},{129,65},{193,129... | collective-permute-start | bytes 786440 | tf_op jit(solution)/shard_map/ppermute | solution.py:320
  197.8 0.0 collective-permute-start
  197.8 11.5 %collective-permute-done.1 = bf16[1,64,2048]{2,1,0:T(8,128)(2,1)S(1)} collective-permute-done((bf16[1,64,2048]{2,1,0:T(8,128)(2,1)S(1)}, bf16[1,64,2048]{2,1,0:T(8,128)(2,1)S(1)}, u32[]{:S(2)}, u32[]{:S(2)}) %collective-permute-start.1) | collective-permute-done | bytes 262176 | tf_op jit(solution)/shard_map/ppermute | solution.py:320
  209.3 4.5 %collective-permute-done = bf16[1,64,2048]{2,1,0:T(8,128)(2,1)S(1)} collective-permute-done((bf16[1,64,2048]{2,1,0:T(8,128)(2,1)S(1)}, bf16[1,64,2048]{2,1,0:T(8,128)(2,1)S(1)}, u32[]{:S(2)}, u32[]{:S(2)}) %collective-permute-start) | collective-permute-done | bytes 262176 | tf_op jit(solution)/shard_map/ppermute | solution.py:320
  213.8 0.7 copy.15
  214.5 0.7 copy.16
  (1 shorter events, 0.0 us)
Async XLA Ops:
  5.7 99.4 %copy-start = (bf16[1,2,2048,384]{3,2,1,0:T(8,128)(2,1)S(1)}, bf16[1,2,2048,384]{3,2,1,0:T(8,128)(2,1)}, u32[]{:S(2)}) copy-start(bf16[1,2,2048,384]{3,2,1,0:T(8,128)(2,1)} %param.19) | copy-start | bytes 9437188
  5.7 99.4 %copy-start.1 = (bf16[1,2,2048,384]{3,2,1,0:T(8,128)(2,1)S(1)}, bf16[1,2,2048,384]{3,2,1,0:T(8,128)(2,1)}, u32[]{:S(2)}) copy-start(bf16[1,2,2048,384]{3,2,1,0:T(8,128)(2,1)} %param.20) | copy-start | bytes 9437188
  5.8 99.4 %copy-start.2 = (bf16[1,2,384,2048]{3,2,1,0:T(8,128)(2,1)S(1)}, bf16[1,2,384,2048]{3,2,1,0:T(8,128)(2,1)}, u32[]{:S(2)}) copy-start(bf16[1,2,384,2048]{3,2,1,0:T(8,128)(2,1)} %param.21) | copy-start | bytes 9437188
  119.7 70.4 %copy-start.3 = (bf16[1,64,2048]{2,1,0:T(8,128)(2,1)S(1)}, bf16[1,64,2048]{2,1,0:T(8,128)(2,1)}, u32[]{:S(2)}) copy-start(bf16[1,64,2048]{2,1,0:T(8,128)(2,1)} %param.11) | copy-start | bytes 786436
  119.7 70.4 %copy-start.4 = (bf16[1,64,2048]{2,1,0:T(8,128)(2,1)S(1)}, bf16[1,64,2048]{2,1,0:T(8,128)(2,1)}, u32[]{:S(2)}) copy-start(bf16[1,64,2048]{2,1,0:T(8,128)(2,1)} %param.14) | copy-start | bytes 786436
  119.7 70.4 %copy-start.5 = (bf16[1,64,2048]{2,1,0:T(8,128)(2,1)S(1)}, bf16[1,64,2048]{2,1,0:T(8,128)(2,1)}, u32[]{:S(2)}) copy-start(bf16[1,64,2048]{2,1,0:T(8,128)(2,1)} %param.15) | copy-start | bytes 786436
  119.7 70.4 %copy-start.6 = (f32[1,2048]{1,0:T(1,128)S(1)}, f32[1,2048]{1,0:T(1,128)}, u32[]{:S(2)}) copy-start(f32[1,2048]{1,0:T(1,128)} %refs_8_.1) | copy-start | bytes 24580
  119.8 70.4 %copy-start.7 = (s32[1,64,8]{1,2,0:T(8,128)S(1)}, s32[1,64,8]{1,2,0:T(8,128)}, u32[]{:S(2)}) copy-start(s32[1,64,8]{1,2,0:T(8,128)} %param.12) | copy-start | bytes 6148
  119.8 70.4 %copy-start.8 = (s32[1,64,8]{1,2,0:T(8,128)S(1)}, s32[1,64,8]{1,2,0:T(8,128)}, u32[]{:S(2)}) copy-start(s32[1,64,8]{1,2,0:T(8,128)} %param.16) | copy-start | bytes 6148
  119.8 70.4 %copy-start.9 = (f32[1,64,8]{1,2,0:T(8,128)S(1)}, f32[1,64,8]{1,2,0:T(8,128)}, u32[]{:S(2)}) copy-start(f32[1,64,8]{1,2,0:T(8,128)} %param.13) | copy-start | bytes 6148
  119.8 70.4 %copy-start.10 = (f32[1,64,8]{1,2,0:T(8,128)S(1)}, f32[1,64,8]{1,2,0:T(8,128)}, u32[]{:S(2)}) copy-start(f32[1,64,8]{1,2,0:T(8,128)} %param.17) | copy-start | bytes 6148
  192.3 17.0 %collective-permute-start.1 = (bf16[1,64,2048]{2,1,0:T(8,128)(2,1)S(1)}, bf16[1,64,2048]{2,1,0:T(8,128)(2,1)S(1)}, u32[]{:S(2)}, u32[]{:S(2)}) collective-permute-start(bf16[1,64,2048]{2,1,0:T(8,128)(2,1)S(1)} %bitcast.35), channel_id=1, source_target_pairs={{0,192},{64,0},{128,64},{192,128},{1,193},{65,1},{129,65},{193,129... | collective-permute-start | bytes 786440 | tf_op jit(solution)/shard_map/ppermute | solution.py:320
  197.8 16.0 %collective-permute-start = (bf16[1,64,2048]{2,1,0:T(8,128)(2,1)S(1)}, bf16[1,64,2048]{2,1,0:T(8,128)(2,1)S(1)}, u32[]{:S(2)}, u32[]{:S(2)}) collective-permute-start(bf16[1,64,2048]{2,1,0:T(8,128)(2,1)S(1)} %bitcast.34), channel_id=1, source_target_pairs={{0,64},{64,128},{128,192},{192,0},{1,65},{65,129},{129,193},{193,1... | collective-permute-start | bytes 786440 | tf_op jit(solution)/shard_map/ppermute | solution.py:320

commit v4 on v3

--- a/solution.py
+++ b/solution.py
@@ -161,45 +161,37 @@
 
 
 def expert_kernel(
-    arrived, w_gate, w_up, down, out, x, ends, gate_up, gu, h, act, grad, lasts, tile, in_sems,
-    out_sems,
+    arrived, w_gate, w_up, down, tile, x, gate_up, gu, h, act, grad, lasts, in_sems
 ):
     local, width, hidden = w_gate.shape
     quarter = width // ROWS
     total = arrived.shape[0]
     groups = total // (local * ROWS)
     bulk = groups * ROWS
-    loads = [pltpu.make_async_copy(arrived.at[:, pl.ds(3 * width, 3 * quarter)], ends, in_sems.at[0])]
-    for block in range(3):
-        loads.append(
+    joins = []
+    for i, source in enumerate((w_gate, w_up)):
+        joins.append(
             pltpu.make_async_copy(
-                arrived.at[:, pl.ds(block * width, width)],
-                x.at[block, pl.ds(0, total), :],
-                in_sems.at[1 + block],
+                source, gate_up.at[:, :, pl.ds(i * hidden, hidden)], in_sems.at[i]
             )
         )
-    for load in loads:
-        load.start()
-    for i, source in enumerate((w_gate, w_up)):
-        loads.append(
-            pltpu.make_async_copy(
-                source, gate_up.at[:, :, pl.ds(i * hidden, hidden)], in_sems.at[4 + i]
-            )
-        )
-        loads[-1].start()
+        joins[i].start()
+
     c = iota((total, total), 1)
     r = iota((total, total), 0)
     where_from = (r % groups) * (local * ROWS) + r // groups
-    loads[0].wait()
-    rest = dot(onehot(c == where_from), ends[...]).astype(BF)
+    rest = dot(onehot(c == where_from), arrived[:, pl.ds(3 * width, 3 * quarter)]).astype(BF)
     for a, e, block, place in (
-        (0, 0, 0, 0), (1, 0, 0, 1), (1, 1, 1, 0), (0, 1, 1, 1), (2, 1, 2, 0), (2, 0, 2, 1),
+        (2, 1, 2, 0), (2, 0, 2, 1), (0, 0, 0, 0), (1, 0, 0, 1), (1, 1, 1, 0), (0, 1, 1, 1),
     ):
         for q in range(ROWS):
             at = (e * ROWS + q) * groups
-            x[block, pl.ds(total + place * groups, groups), pl.ds(q * quarter, quarter)] = rest[
+            x[block, pl.ds(place * groups, groups), pl.ds(q * quarter, quarter)] = rest[
                 at : at + groups, a * quarter : (a + 1) * quarter
             ]
+
+    def rows_of(block):
+        return jnp.concatenate([arrived[:, pl.ds(block * width, width)], x[block]], axis=0)
 
     step = 2 * hidden // 3
     third = hidden // 3
@@ -207,7 +199,7 @@
     def gate_up_of(e):
         for n in range(3):
             cols = pl.ds(n * step, step)
-            gu[e, :, cols] = dot(x[e], gate_up[e, :, cols])
+            gu[e, :, cols] = dot(rows_of(e), gate_up[e, :, cols])
 
     def take(values, e, forward):
         upper = forward == (e == 1)
@@ -230,14 +222,7 @@
             grad[e, :, pl.ds(at, third)] = (b * u * s * (1.0 + g * (1.0 - s))).astype(BF)
             grad[e, :, pl.ds(hidden + at, third)] = (b * g * s).astype(BF)
 
-    copies = []
     back_to = onehot(r == (c % groups) * (local * ROWS) + c // groups)
-
-    def ship(at):
-        cols = pl.ds(at * quarter, quarter)
-        copy = pltpu.make_async_copy(tile.at[:, cols], out.at[:, cols], out_sems.at[at])
-        copy.start()
-        copies.append(copy)
 
     def send_back(a, q):
         part = pl.ds(q * quarter, quarter)
@@ -250,23 +235,20 @@
             lasts[pl.ds((e * ROWS + q) * groups, groups), pl.ds(a * quarter, quarter)] = o[e][
                 bulk:
             ].astype(BF)
-        ship(a * ROWS + q)
 
     def send_back_last(a):
         tile[:, pl.ds((2 * ROWS + a) * quarter, quarter)] = dot(
             back_to, lasts[:, pl.ds(a * quarter, quarter)]
         ).astype(BF)
-        ship(2 * ROWS + a)
-
-    for load in loads[1:3] + loads[4:]:
-        load.wait()
+
+    for n in range(3):
+        cols = pl.ds(n * step, step)
+        h[:, cols] = dot(rows_of(2), down[cols, :], NT)
+    for join in joins:
+        join.wait()
     gate_up_of(0)
     gate_up_of(1)
     forward_of(0)
-    loads[3].wait()
-    for n in range(3):
-        cols = pl.ds(n * step, step)
-        h[:, cols] = dot(x[2], down[cols, :], NT)
     forward_of(1)
     for q in range(ROWS):
         send_back(0, q)
@@ -276,8 +258,6 @@
     for q in range(ROWS):
         send_back(1, q)
     send_back_last(1)
-    for copy in copies:
-        copy.wait()
 
 
 def weighted_sum(part, returned, matrix):
@@ -374,22 +354,19 @@
     worked = pl.pallas_call(
         expert_kernel,
         out_shape=jax.ShapeDtypeStruct((rows, 2 * wide), BF),
-        in_specs=[hbm] + [vmem] * 3,
-        out_specs=hbm,
+        in_specs=[vmem] * 4,
+        out_specs=vmem,
         scratch_shapes=[
-            pltpu.VMEM((3, total, width), BF),
-            pltpu.VMEM((rows, 3 * quarter), BF),
+            pltpu.VMEM((3, 2 * group, width), BF),
             pltpu.VMEM((local, width, 2 * hidden), BF),
             pltpu.VMEM((local, total, 2 * hidden), F32),
             pltpu.VMEM((total, local * hidden), F32),
             pltpu.VMEM((local, bulk + group, hidden), BF),
             pltpu.VMEM((local, bulk + group, 2 * hidden), BF),
             pltpu.VMEM((rows, 2 * quarter), BF),
-            pltpu.VMEM((rows, 2 * wide), BF),
-            pltpu.SemaphoreType.DMA((6,)),
-            pltpu.SemaphoreType.DMA((2 * ROWS + 2,)),
+            pltpu.SemaphoreType.DMA((2,)),
         ],
-        compiler_params=pltpu.CompilerParams(vmem_limit_bytes=40 * 1024 * 1024),
+        compiler_params=pltpu.CompilerParams(vmem_limit_bytes=28 * 1024 * 1024),
         cost_estimate=cost(20e9, 22e6),
         name="experts",
     )(

time: 216 us -> 214 us (level)
  no operation moved by 1% of the time
where the time goes in v4:
time: 214 us
  blocking collectives  169 us (79%)
  Pallas kernels  20.8 us (10%)
  waiting for transfers between devices  16 us (7%)
  starting transfers between devices  5.49 us (3%)
    all_to_all x2, blocking collectives, exchange(): lax.all_to_all(packed, ('dp', 'expert'), split_axis=0, concat_axis=0, til...  169 us
    ppermute x2, waiting for transfers between devices, from_behind(): return lax.ppermute(value, axis, pairs)  16 us
    pallas_call x1, Pallas kernels, body(): pl.pallas_call(expert_kernel, out_shape=jax.ShapeDtypeStruct((rows, 2 * w...  13.5 us
    ppermute x2, starting transfers between devices, from_behind(): return lax.ppermute(value, axis, pairs)  5.49 us
    pallas_call x1, Pallas kernels, body(): pl.pallas_call(lambda *refs: pack_kernel(experts, *refs), out_shape=jax.S...  5.06 us
  transfers between devices with their start and end apart: 2, of which 2 were waited for; matrix products, arithmetic and copies ran while one was open for 0% of the time, Pallas kernels for 0%

profile of v4, /device:TPU:32, one launch (start us, length us, event | category | flops | bytes accessed | tf_op | source)
XLA Modules:
  0.0 213.9 jit_solution(7267984933307711157)
XLA Ops:
  0.6 5.1 %pack.1 = bf16[512,7680]{1,0:T(8,128)(2,1)} custom-call(bf16[64,2048]{1,0:T(8,128)(2,1)} %bitcast.30, bf16[64,2048]{1,0:T(8,128)(2,1)} %bitcast.32, bf16[64,2048]{1,0:T(8,128)(2,1)} %bitcast.34, s32[8,64]{1,0:T(8,128)} %bitcast.38, s32[8,64]{1,0:T(8,128)} %bitcast.40, f32[1,2048]{1,0:T(1,128)} %refs_8_.1), custom_call_target="tpu_custom_call" | custom-call | flops 8999999488 | bytes 9000000 | tf_op jit(solution)/shard_map/pack/pallas_call | solution.py:339
  5.7 0.0 copy-start
  5.7 0.0 copy-start.1
  5.7 0.0 copy-start.2
  5.7 99.3 %all_to_all.22 = bf16[64,8,7680]{2,1,0:T(8,128)(2,1)S(1)} all-to-all(bf16[64,8,7680]{2,1,0:T(8,128)(2,1)} %bitcast.44), channel_id=1, replica_groups=mesh['segment'=4,'dp'=4,'expert'=16] {'dp','expert'}, dimensions={0} | all-to-all | bytes 15728640 | tf_op jit(solution)/shard_map/all_to_all | solution.py:337
  105.0 0.0 copy-done
  105.0 0.0 copy-done.1
  105.0 0.0 copy-done.2
  105.0 13.5 %experts.1 = bf16[512,5120]{1,0:T(8,128)(2,1)S(1)} custom-call(bf16[512,7680]{1,0:T(8,128)(2,1)S(1)} %bitcast.24, bf16[2,2048,384]{2,1,0:T(8,128)(2,1)S(1)} %bitcast.27, bf16[2,2048,384]{2,1,0:T(8,128)(2,1)S(1)} %bitcast.28, bf16[768,2048]{1,0:T(8,128)(2,1)S(1)} %bitcast.29), custom_call_target="tpu_custom_call" | custom-call | flops 20000000000 | bytes 22000000 | tf_op jit(solution)/shard_map/experts/pallas_call | solution.py:354
  118.6 0.0 copy-start.3
  118.6 0.0 copy-start.4
  118.6 0.0 copy-start.5
  118.6 0.0 copy-start.6
  118.7 0.0 copy-start.7
  118.7 0.0 copy-start.8
  118.7 0.0 copy-start.9
  118.7 0.0 copy-start.10
  118.7 70.1 %all_to_all.23 = bf16[64,8,5120]{2,1,0:T(8,128)(2,1)S(1)} all-to-all(bf16[64,8,5120]{2,1,0:T(8,128)(2,1)S(1)} %bitcast.26), channel_id=1, replica_groups=mesh['segment'=4,'dp'=4,'expert'=16] {'dp','expert'}, dimensions={0} | all-to-all | bytes 10485760 | tf_op jit(solution)/shard_map/all_to_all | solution.py:337
  188.8 0.0 copy-done.3
  188.8 0.0 copy-done.4
  188.8 0.0 copy-done.5
  188.8 0.0 copy-done.6
  188.8 0.0 copy-done.7
  188.8 0.0 copy-done.8
  188.8 0.0 copy-done.9
  188.8 2.2 %combine.1 = (bf16[64,2048]{1,0:T(8,128)(2,1)S(1)}, bf16[64,2048]{1,0:T(8,128)(2,1)S(1)}) custom-call(bf16[512,5120]{1,0:T(8,128)(2,1)S(1)} %bitcast.25, s32[8,64]{1,0:T(8,128)S(1)} %bitcast.39, s32[8,64]{1,0:T(8,128)S(1)} %bitcast.41, f32[8,64]{1,0:T(8,128)S(1)} %bitcast.42, f32[8,64]{1,0:T(8,128)S(1)} %bitcast.43, bf16[64,2048]{1,0:T(8,128)(2,1)S(1)} %bitcast.33, ...), custom_call_target="tpu_custom_call" | custom-call | flops 4000000000 | bytes 8000000 | tf_op jit(solution)/shard_map/combine/pallas_call | solution.py:381
  191.0 5.5 %collective-permute-start.1 = (bf16[1,64,2048]{2,1,0:T(8,128)(2,1)S(1)}, bf16[1,64,2048]{2,1,0:T(8,128)(2,1)S(1)}, u32[]{:S(2)}, u32[]{:S(2)}) collective-permute-start(bf16[1,64,2048]{2,1,0:T(8,128)(2,1)S(1)} %bitcast.37), channel_id=1, source_target_pairs={{0,192},{64,0},{128,64},{192,128},{1,193},{65,1},{129,65},{193,129... | collective-permute-start | bytes 786440 | tf_op jit(solution)/shard_map/ppermute | solution.py:300
  196.5 0.0 collective-permute-start
  196.5 11.5 %collective-permute-done.1 = bf16[1,64,2048]{2,1,0:T(8,128)(2,1)S(1)} collective-permute-done((bf16[1,64,2048]{2,1,0:T(8,128)(2,1)S(1)}, bf16[1,64,2048]{2,1,0:T(8,128)(2,1)S(1)}, u32[]{:S(2)}, u32[]{:S(2)}) %collective-permute-start.1) | collective-permute-done | bytes 262176 | tf_op jit(solution)/shard_map/ppermute | solution.py:300
  208.0 4.5 %collective-permute-done = bf16[1,64,2048]{2,1,0:T(8,128)(2,1)S(1)} collective-permute-done((bf16[1,64,2048]{2,1,0:T(8,128)(2,1)S(1)}, bf16[1,64,2048]{2,1,0:T(8,128)(2,1)S(1)}, u32[]{:S(2)}, u32[]{:S(2)}) %collective-permute-start) | collective-permute-done | bytes 262176 | tf_op jit(solution)/shard_map/ppermute | solution.py:300
  212.5 0.7 copy.15
  213.2 0.7 copy.16
  (1 shorter events, 0.0 us)
Async XLA Ops:
  5.7 99.3 %copy-start = (bf16[1,2,2048,384]{3,2,1,0:T(8,128)(2,1)S(1)}, bf16[1,2,2048,384]{3,2,1,0:T(8,128)(2,1)}, u32[]{:S(2)}) copy-start(bf16[1,2,2048,384]{3,2,1,0:T(8,128)(2,1)} %param.19) | copy-start | bytes 9437188
  5.7 99.3 %copy-start.1 = (bf16[1,2,2048,384]{3,2,1,0:T(8,128)(2,1)S(1)}, bf16[1,2,2048,384]{3,2,1,0:T(8,128)(2,1)}, u32[]{:S(2)}) copy-start(bf16[1,2,2048,384]{3,2,1,0:T(8,128)(2,1)} %param.20) | copy-start | bytes 9437188
  5.7 99.3 %copy-start.2 = (bf16[1,2,384,2048]{3,2,1,0:T(8,128)(2,1)S(1)}, bf16[1,2,384,2048]{3,2,1,0:T(8,128)(2,1)}, u32[]{:S(2)}) copy-start(bf16[1,2,384,2048]{3,2,1,0:T(8,128)(2,1)} %param.21) | copy-start | bytes 9437188
  118.6 70.2 %copy-start.3 = (bf16[1,64,2048]{2,1,0:T(8,128)(2,1)S(1)}, bf16[1,64,2048]{2,1,0:T(8,128)(2,1)}, u32[]{:S(2)}) copy-start(bf16[1,64,2048]{2,1,0:T(8,128)(2,1)} %param.11) | copy-start | bytes 786436
  118.6 70.2 %copy-start.4 = (bf16[1,64,2048]{2,1,0:T(8,128)(2,1)S(1)}, bf16[1,64,2048]{2,1,0:T(8,128)(2,1)}, u32[]{:S(2)}) copy-start(bf16[1,64,2048]{2,1,0:T(8,128)(2,1)} %param.14) | copy-start | bytes 786436
  118.6 70.2 %copy-start.5 = (bf16[1,64,2048]{2,1,0:T(8,128)(2,1)S(1)}, bf16[1,64,2048]{2,1,0:T(8,128)(2,1)}, u32[]{:S(2)}) copy-start(bf16[1,64,2048]{2,1,0:T(8,128)(2,1)} %param.15) | copy-start | bytes 786436
  118.6 70.1 %copy-start.6 = (f32[1,2048]{1,0:T(1,128)S(1)}, f32[1,2048]{1,0:T(1,128)}, u32[]{:S(2)}) copy-start(f32[1,2048]{1,0:T(1,128)} %refs_8_.1) | copy-start | bytes 24580
  118.7 70.1 %copy-start.7 = (s32[1,64,8]{1,2,0:T(8,128)S(1)}, s32[1,64,8]{1,2,0:T(8,128)}, u32[]{:S(2)}) copy-start(s32[1,64,8]{1,2,0:T(8,128)} %param.12) | copy-start | bytes 6148
  118.7 70.1 %copy-start.8 = (s32[1,64,8]{1,2,0:T(8,128)S(1)}, s32[1,64,8]{1,2,0:T(8,128)}, u32[]{:S(2)}) copy-start(s32[1,64,8]{1,2,0:T(8,128)} %param.16) | copy-start | bytes 6148
  118.7 70.1 %copy-start.9 = (f32[1,64,8]{1,2,0:T(8,128)S(1)}, f32[1,64,8]{1,2,0:T(8,128)}, u32[]{:S(2)}) copy-start(f32[1,64,8]{1,2,0:T(8,128)} %param.13) | copy-start | bytes 6148
  118.7 70.1 %copy-start.10 = (f32[1,64,8]{1,2,0:T(8,128)S(1)}, f32[1,64,8]{1,2,0:T(8,128)}, u32[]{:S(2)}) copy-start(f32[1,64,8]{1,2,0:T(8,128)} %param.17) | copy-start | bytes 6148
  191.0 17.0 %collective-permute-start.1 = (bf16[1,64,2048]{2,1,0:T(8,128)(2,1)S(1)}, bf16[1,64,2048]{2,1,0:T(8,128)(2,1)S(1)}, u32[]{:S(2)}, u32[]{:S(2)}) collective-permute-start(bf16[1,64,2048]{2,1,0:T(8,128)(2,1)S(1)} %bitcast.37), channel_id=1, source_target_pairs={{0,192},{64,0},{128,64},{192,128},{1,193},{65,1},{129,65},{193,129... | collective-permute-start | bytes 786440 | tf_op jit(solution)/shard_map/ppermute | solution.py:300
  196.5 16.0 %collective-permute-start = (bf16[1,64,2048]{2,1,0:T(8,128)(2,1)S(1)}, bf16[1,64,2048]{2,1,0:T(8,128)(2,1)S(1)}, u32[]{:S(2)}, u32[]{:S(2)}) collective-permute-start(bf16[1,64,2048]{2,1,0:T(8,128)(2,1)S(1)} %bitcast.36), channel_id=1, source_target_pairs={{0,64},{64,128},{128,192},{192,0},{1,65},{65,129},{129,193},{193,1... | collective-permute-start | bytes 786440 | tf_op jit(solution)/shard_map/ppermute | solution.py:300

commit v5 on v4

--- a/solution.py
+++ b/solution.py
@@ -11,6 +11,7 @@
 F32 = jnp.float32
 SLOTS = 5
 ROWS = 4
+LOCAL = 2
 NN = (((1,), (0,)), ((), ()))
 NT = (((1,), (1,)), ((), ()))
 TN = (((0,), (0,)), ((), ()))
@@ -28,9 +29,16 @@
     return jnp.where(mask, 1.0, 0.0).astype(BF)
 
 
+def wire_ids(experts, tokens):
+    at = iota((experts, tokens), 0)
+    count = lax.axis_size("dp")
+    device = (at // LOCAL) % count * (experts // LOCAL // count) + at // LOCAL // count
+    return device * LOCAL + at % LOCAL
+
+
 def slot_marks(routes, experts):
     top, tokens = routes.shape
-    ids = iota((experts, tokens), 0)
+    ids = wire_ids(experts, tokens)
     member = jnp.zeros((experts, tokens), F32)
     for k in range(top):
         member = jnp.where(routes[k : k + 1] == ids, 1.0, member)
@@ -113,7 +121,7 @@
 def weight_matrix(routes, weights, experts):
     top, tokens = routes.shape
     rows = experts * ROWS
-    ids = iota((experts, tokens), 0)
+    ids = wire_ids(experts, tokens)
     factor = jnp.zeros((experts, tokens), F32)
     for k in range(top):
         factor = jnp.where(routes[k : k + 1] == ids, weights[k : k + 1], factor)
@@ -334,7 +342,7 @@
         return pl.CostEstimate(flops=int(flops), bytes_accessed=int(moved), transcendentals=0)
 
     def exchange(packed):
-        return lax.all_to_all(packed, ("dp", "expert"), split_axis=0, concat_axis=0, tiled=True)
+        return lax.all_to_all(packed, ("expert", "dp"), split_axis=0, concat_axis=0, tiled=True)
 
     packed = pl.pallas_call(
         lambda *refs: pack_kernel(experts, *refs),

time: 214 us -> 211 us (0.986)
    all_to_all x2, blocking collectives: 169 us -> 167 us  [exchange(): lax.all_to_all(packed, ('expert', 'dp'), split_axis=0, concat_axis=0, til...]
where the time goes in v5:
time: 211 us
  blocking collectives  167 us (79%)
  Pallas kernels  20.8 us (10%)
  waiting for transfers between devices  15.4 us (7%)
  starting transfers between devices  5.48 us (3%)
    all_to_all x2, blocking collectives, exchange(): lax.all_to_all(packed, ('expert', 'dp'), split_axis=0, concat_axis=0, til...  167 us
    ppermute x2, waiting for transfers between devices, from_behind(): return lax.ppermute(value, axis, pairs)  15.4 us
    pallas_call x1, Pallas kernels, body(): pl.pallas_call(expert_kernel, out_shape=jax.ShapeDtypeStruct((rows, 2 * w...  13.5 us
    ppermute x2, starting transfers between devices, from_behind(): return lax.ppermute(value, axis, pairs)  5.48 us
    pallas_call x1, Pallas kernels, body(): pl.pallas_call(lambda *refs: pack_kernel(experts, *refs), out_shape=jax.S...  5.08 us
  transfers between devices with their start and end apart: 2, of which 2 were waited for; matrix products, arithmetic and copies ran while one was open for 0% of the time, Pallas kernels for 0%

profile of v5, /device:TPU:32, one launch (start us, length us, event | category | flops | bytes accessed | tf_op | source)
XLA Modules:
  0.0 210.9 jit_solution(8696722662446691162)
XLA Ops:
  0.6 5.1 %pack.1 = bf16[512,7680]{1,0:T(8,128)(2,1)} custom-call(bf16[64,2048]{1,0:T(8,128)(2,1)} %bitcast.30, bf16[64,2048]{1,0:T(8,128)(2,1)} %bitcast.32, bf16[64,2048]{1,0:T(8,128)(2,1)} %bitcast.34, s32[8,64]{1,0:T(8,128)} %bitcast.38, s32[8,64]{1,0:T(8,128)} %bitcast.40, f32[1,2048]{1,0:T(1,128)} %refs_8_.1), custom_call_target="tpu_custom_call" | custom-call | flops 8999999488 | bytes 9000000 | tf_op jit(solution)/shard_map/pack/pallas_call | solution.py:347
  5.7 0.0 copy-start
  5.7 0.0 copy-start.1
  5.7 0.0 copy-start.2
  5.8 99.7 %all_to_all.22 = bf16[64,8,7680]{2,1,0:T(8,128)(2,1)S(1)} all-to-all(bf16[64,8,7680]{2,1,0:T(8,128)(2,1)} %bitcast.44), channel_id=1, replica_groups=mesh['segment'=4,'dp'=4,'expert'=16] {'expert','dp'}, dimensions={0} | all-to-all | bytes 15728640 | tf_op jit(solution)/shard_map/all_to_all | solution.py:345
  105.5 0.0 copy-done
  105.5 0.0 copy-done.1
  105.5 0.0 copy-done.2
  105.5 13.5 %experts.1 = bf16[512,5120]{1,0:T(8,128)(2,1)S(1)} custom-call(bf16[512,7680]{1,0:T(8,128)(2,1)S(1)} %bitcast.24, bf16[2,2048,384]{2,1,0:T(8,128)(2,1)S(1)} %bitcast.27, bf16[2,2048,384]{2,1,0:T(8,128)(2,1)S(1)} %bitcast.28, bf16[768,2048]{1,0:T(8,128)(2,1)S(1)} %bitcast.29), custom_call_target="tpu_custom_call" | custom-call | flops 20000000000 | bytes 22000000 | tf_op jit(solution)/shard_map/experts/pallas_call | solution.py:362
  119.0 0.0 copy-start.3
  119.1 0.0 copy-start.4
  119.1 0.0 copy-start.5
  119.1 0.0 copy-start.6
  119.1 0.0 copy-start.7
  119.1 0.0 copy-start.8
  119.1 0.0 copy-start.9
  119.1 0.0 copy-start.10
  119.1 67.3 %all_to_all.23 = bf16[64,8,5120]{2,1,0:T(8,128)(2,1)S(1)} all-to-all(bf16[64,8,5120]{2,1,0:T(8,128)(2,1)S(1)} %bitcast.26), channel_id=1, replica_groups=mesh['segment'=4,'dp'=4,'expert'=16] {'expert','dp'}, dimensions={0} | all-to-all | bytes 10485760 | tf_op jit(solution)/shard_map/all_to_all | solution.py:345
  186.5 0.0 copy-done.3
  186.5 0.0 copy-done.4
  186.5 0.0 copy-done.5
  186.5 0.0 copy-done.6
  186.5 0.0 copy-done.7
  186.5 0.0 copy-done.8
  186.5 0.0 copy-done.9
  186.5 2.1 %combine.1 = (bf16[64,2048]{1,0:T(8,128)(2,1)S(1)}, bf16[64,2048]{1,0:T(8,128)(2,1)S(1)}) custom-call(bf16[512,5120]{1,0:T(8,128)(2,1)S(1)} %bitcast.25, s32[8,64]{1,0:T(8,128)S(1)} %bitcast.39, s32[8,64]{1,0:T(8,128)S(1)} %bitcast.41, f32[8,64]{1,0:T(8,128)S(1)} %bitcast.42, f32[8,64]{1,0:T(8,128)S(1)} %bitcast.43, bf16[64,2048]{1,0:T(8,128)(2,1)S(1)} %bitcast.33, ...), custom_call_target="tpu_custom_call" | custom-call | flops 4000000000 | bytes 8000000 | tf_op jit(solution)/shard_map/combine/pallas_call | solution.py:389
  188.7 5.5 %collective-permute-start.1 = (bf16[1,64,2048]{2,1,0:T(8,128)(2,1)S(1)}, bf16[1,64,2048]{2,1,0:T(8,128)(2,1)S(1)}, u32[]{:S(2)}, u32[]{:S(2)}) collective-permute-start(bf16[1,64,2048]{2,1,0:T(8,128)(2,1)S(1)} %bitcast.37), channel_id=1, source_target_pairs={{0,192},{64,0},{128,64},{192,128},{1,193},{65,1},{129,65},{193,129... | collective-permute-start | bytes 786440 | tf_op jit(solution)/shard_map/ppermute | solution.py:308
  194.2 0.0 collective-permute-start
  194.2 10.3 %collective-permute-done.1 = bf16[1,64,2048]{2,1,0:T(8,128)(2,1)S(1)} collective-permute-done((bf16[1,64,2048]{2,1,0:T(8,128)(2,1)S(1)}, bf16[1,64,2048]{2,1,0:T(8,128)(2,1)S(1)}, u32[]{:S(2)}, u32[]{:S(2)}) %collective-permute-start.1) | collective-permute-done | bytes 262176 | tf_op jit(solution)/shard_map/ppermute | solution.py:308
  204.5 5.1 %collective-permute-done = bf16[1,64,2048]{2,1,0:T(8,128)(2,1)S(1)} collective-permute-done((bf16[1,64,2048]{2,1,0:T(8,128)(2,1)S(1)}, bf16[1,64,2048]{2,1,0:T(8,128)(2,1)S(1)}, u32[]{:S(2)}, u32[]{:S(2)}) %collective-permute-start) | collective-permute-done | bytes 262176 | tf_op jit(solution)/shard_map/ppermute | solution.py:308
  209.5 0.7 copy.15
  210.2 0.7 copy.16
  (1 shorter events, 0.0 us)
Async XLA Ops:
  5.7 99.8 %copy-start = (bf16[1,2,2048,384]{3,2,1,0:T(8,128)(2,1)S(1)}, bf16[1,2,2048,384]{3,2,1,0:T(8,128)(2,1)}, u32[]{:S(2)}) copy-start(bf16[1,2,2048,384]{3,2,1,0:T(8,128)(2,1)} %param.19) | copy-start | bytes 9437188
  5.7 99.7 %copy-start.1 = (bf16[1,2,2048,384]{3,2,1,0:T(8,128)(2,1)S(1)}, bf16[1,2,2048,384]{3,2,1,0:T(8,128)(2,1)}, u32[]{:S(2)}) copy-start(bf16[1,2,2048,384]{3,2,1,0:T(8,128)(2,1)} %param.20) | copy-start | bytes 9437188
  5.7 99.7 %copy-start.2 = (bf16[1,2,384,2048]{3,2,1,0:T(8,128)(2,1)S(1)}, bf16[1,2,384,2048]{3,2,1,0:T(8,128)(2,1)}, u32[]{:S(2)}) copy-start(bf16[1,2,384,2048]{3,2,1,0:T(8,128)(2,1)} %param.21) | copy-start | bytes 9437188
  119.0 67.4 %copy-start.3 = (bf16[1,64,2048]{2,1,0:T(8,128)(2,1)S(1)}, bf16[1,64,2048]{2,1,0:T(8,128)(2,1)}, u32[]{:S(2)}) copy-start(bf16[1,64,2048]{2,1,0:T(8,128)(2,1)} %param.11) | copy-start | bytes 786436
  119.1 67.4 %copy-start.4 = (bf16[1,64,2048]{2,1,0:T(8,128)(2,1)S(1)}, bf16[1,64,2048]{2,1,0:T(8,128)(2,1)}, u32[]{:S(2)}) copy-start(bf16[1,64,2048]{2,1,0:T(8,128)(2,1)} %param.14) | copy-start | bytes 786436
  119.1 67.4 %copy-start.5 = (bf16[1,64,2048]{2,1,0:T(8,128)(2,1)S(1)}, bf16[1,64,2048]{2,1,0:T(8,128)(2,1)}, u32[]{:S(2)}) copy-start(bf16[1,64,2048]{2,1,0:T(8,128)(2,1)} %param.15) | copy-start | bytes 786436
  119.1 67.4 %copy-start.6 = (f32[1,2048]{1,0:T(1,128)S(1)}, f32[1,2048]{1,0:T(1,128)}, u32[]{:S(2)}) copy-start(f32[1,2048]{1,0:T(1,128)} %refs_8_.1) | copy-start | bytes 24580
  119.1 67.4 %copy-start.7 = (s32[1,64,8]{1,2,0:T(8,128)S(1)}, s32[1,64,8]{1,2,0:T(8,128)}, u32[]{:S(2)}) copy-start(s32[1,64,8]{1,2,0:T(8,128)} %param.12) | copy-start | bytes 6148
  119.1 67.4 %copy-start.8 = (s32[1,64,8]{1,2,0:T(8,128)S(1)}, s32[1,64,8]{1,2,0:T(8,128)}, u32[]{:S(2)}) copy-start(s32[1,64,8]{1,2,0:T(8,128)} %param.16) | copy-start | bytes 6148
  119.1 67.4 %copy-start.9 = (f32[1,64,8]{1,2,0:T(8,128)S(1)}, f32[1,64,8]{1,2,0:T(8,128)}, u32[]{:S(2)}) copy-start(f32[1,64,8]{1,2,0:T(8,128)} %param.13) | copy-start | bytes 6148
  119.1 67.4 %copy-start.10 = (f32[1,64,8]{1,2,0:T(8,128)S(1)}, f32[1,64,8]{1,2,0:T(8,128)}, u32[]{:S(2)}) copy-start(f32[1,64,8]{1,2,0:T(8,128)} %param.17) | copy-start | bytes 6148
  188.7 15.8 %collective-permute-start.1 = (bf16[1,64,2048]{2,1,0:T(8,128)(2,1)S(1)}, bf16[1,64,2048]{2,1,0:T(8,128)(2,1)S(1)}, u32[]{:S(2)}, u32[]{:S(2)}) collective-permute-start(bf16[1,64,2048]{2,1,0:T(8,128)(2,1)S(1)} %bitcast.37), channel_id=1, source_target_pairs={{0,192},{64,0},{128,64},{192,128},{1,193},{65,1},{129,65},{193,129... | collective-permute-start | bytes 786440 | tf_op jit(solution)/shard_map/ppermute | solution.py:308
  194.2 15.4 %collective-permute-start = (bf16[1,64,2048]{2,1,0:T(8,128)(2,1)S(1)}, bf16[1,64,2048]{2,1,0:T(8,128)(2,1)S(1)}, u32[]{:S(2)}, u32[]{:S(2)}) collective-permute-start(bf16[1,64,2048]{2,1,0:T(8,128)(2,1)S(1)} %bitcast.36), channel_id=1, source_target_pairs={{0,64},{64,128},{128,192},{192,0},{1,65},{65,129},{129,193},{193,1... | collective-permute-start | bytes 786440 | tf_op jit(solution)/shard_map/ppermute | solution.py:308
